TPU v7x, 512 devices: a whole 4x8x8 slice. The times are simulated.
512 devices in a mesh: ctx: 16 (over y, core), head: 4 (over x), dp: 8 (over z).
Axes of the slice: x: 4, y: 8, z: 8, core: 2. Of those that a mesh axis runs over, the one named last changes fastest.
Arguments:
- x_query: bfloat16 [8, 8192, 2560], P('dp', ('ctx', 'head')), may hold values from -6 to 6
- x_key: bfloat16 [8, 8192, 2560], P('dp', ('ctx', 'head')), may hold values from -7 to 7
- values: bfloat16 [8, 8192, 2560], P('dp', ('ctx', 'head')), may hold values from -6 to 6
- grad_out: bfloat16 [8, 8192, 2560], P('dp', ('ctx', 'head')), may hold values from -6 to 6
- gain_query: float32 [2560], replicated, may hold values from 0.5 to 1.5
- gain_key: float32 [2560], replicated, may hold values from 0.5 to 1.5
- key_tiles: int32 [8, 128, 6], P('dp'), may hold values from 0 to 127, as said below
Outputs:
- grad_x_query: bfloat16 [8, 8192, 2560], P('dp', ('ctx', 'head'))
- grad_x_key: bfloat16 [8, 8192, 2560], P('dp', ('ctx', 'head'))
- grad_values: bfloat16 [8, 8192, 2560], P('dp', ('ctx', 'head'))
- grad_gain_query: float32 [2560], replicated
- grad_gain_key: float32 [2560], replicated
Inputs may be any that keep to these rules, and one draw needn't show every extreme that they name: `key_tiles`: each row lists 6 distinct tiles. Tiles are grouped in blocks of 8 consecutive tiles; a query tile lists only tiles of its own block and of the blocks just before and after it. The query tiles of one block together list every tile of their own block and exactly 4 distinct tiles of each block beside it.
All inputs are finite; a program needn't handle non-finite values.
Results may differ from a plain program's by a relative error of at most 0.02.
Values may be sent and summed in bfloat16 or wider, within the bound.
No kernel may reach another device: no remote copies, remote signals or barrier semaphores. Data moves between devices by JAX's collectives and lax.ppermute only.
A program may use at most 128 MiB of HBM per device.

v0:
```python
import jax
import jax.numpy as jnp
from jax import lax
from jax.experimental import pallas as pl
from jax.experimental.pallas import tpu as pltpu
from jax.sharding import PartitionSpec as P

HD = 128
TILE = 64
ROWS = 16
FAR = -(1 << 20)
GROUP = 4
SIDE = 4

epsilon = 1e-06


def cost(flops, moved, exps=0):
    return pl.CostEstimate(flops=flops, bytes_accessed=moved, transcendentals=exps)


def plan_kernel(listed_ref, plan_ref, slot_ref, *, blocks, listed):
    count = blocks * listed

    def bits(start):
        def step(i, mask):
            tile = listed_ref[start + i]
            inside = jnp.logical_and(tile >= -blocks, tile < 2 * blocks)
            bit = lax.shift_left(jnp.int32(1), jnp.where(inside, tile + blocks, 0))
            return mask | jnp.where(inside, bit, 0)

        return lax.fori_loop(0, count, step, jnp.int32(0))

    before, own, after = bits(0), bits(count), bits(2 * count)
    for i in range(16):
        plan_ref[count + i] = 0
    low, high, to_after, to_before = (jnp.int32(0),) * 4
    for b in range(blocks):
        slot_ref[b] = blocks + low
        slot_ref[blocks + b] = jnp.int32(b)
        slot_ref[2 * blocks + b] = blocks + SIDE + high
        low += lax.shift_right_logical(own, jnp.int32(b)) & 1
        high += lax.shift_right_logical(own, jnp.int32(2 * blocks + b)) & 1
        plan_ref[count + to_after] = jnp.int32(b)
        to_after += lax.shift_right_logical(after, jnp.int32(blocks + b)) & 1
        plan_ref[count + 8 + to_before] = jnp.int32(b)
        to_before += lax.shift_right_logical(before, jnp.int32(blocks + b)) & 1

    def place(i, carry):
        tile = jnp.clip(listed_ref[count + i], -blocks, 2 * blocks - 1)
        plan_ref[i] = slot_ref[tile + blocks]
        return carry

    lax.fori_loop(0, count, place, jnp.int32(0))


def make_plan(key_tiles, blocks):
    listed = key_tiles.shape[2]
    start = lax.axis_index("ctx") * blocks
    padded = jnp.pad(key_tiles[0] - start, ((blocks, blocks), (0, 0)), constant_values=FAR)
    near = lax.dynamic_slice_in_dim(padded, start, 3 * blocks, 0).reshape(-1)
    count = blocks * listed
    return pl.pallas_call(
        lambda a, b, c: plan_kernel(a, b, c, blocks=blocks, listed=listed),
        out_shape=jax.ShapeDtypeStruct((count + 16,), jnp.int32),
        in_specs=[pl.BlockSpec(memory_space=pltpu.SMEM)],
        out_specs=pl.BlockSpec(memory_space=pltpu.SMEM),
        scratch_shapes=[pltpu.SMEM((3 * blocks,), jnp.int32)],
        cost_estimate=cost(1000, 1000),
        name="plan",
    )(near)


def norm_kernel(x_ref, y_ref, gain_ref, out_ref, *, groups, heads):
    width = groups * heads * HD

    def step(c, carry):
        rows = pl.ds(c * ROWS, ROWS)
        x = x_ref[rows, :].astype(jnp.float32)
        scaling = lax.rsqrt(jnp.sum(x * x, axis=-1, keepdims=True) / width + epsilon)
        for g in range(groups):
            for h in range(heads):
                cols = slice((g * heads + h) * HD, (g * heads + h + 1) * HD)
                part = x_ref[rows, cols].astype(jnp.float32) * scaling * gain_ref[:, cols]
                out_ref[g, 0, h, 0, rows, :] = part.astype(jnp.bfloat16)
                out_ref[g, 1, h, 0, rows, :] = y_ref[rows, cols]
        return carry

    lax.fori_loop(0, TILE // ROWS, step, 0)


def norm_pack(x, y, gain, groups, name):
    tokens, width = x.shape
    heads = width // HD // groups
    tiles = tokens // TILE
    return pl.pallas_call(
        lambda *refs: norm_kernel(*refs, groups=groups, heads=heads),
        grid=(tiles,),
        out_shape=jax.ShapeDtypeStruct((groups, 2, heads, tiles, TILE, HD), jnp.bfloat16),
        in_specs=[
            pl.BlockSpec((TILE, width), lambda i: (i, 0)),
            pl.BlockSpec((TILE, width), lambda i: (i, 0)),
            pl.BlockSpec((1, width), lambda i: (0, 0)),
        ],
        out_specs=pl.BlockSpec(
            (groups, 2, heads, 1, TILE, HD), lambda i: (0, 0, 0, i, 0, 0)
        ),
        cost_estimate=cost(8 * tokens * width, 8 * tokens * width),
        name=name,
    )(x, y, gain.reshape(1, width))


def unnorm_kernel(x_ref, back_ref, gain_ref, out_ref, *rest, groups, heads):
    width = groups * heads * HD
    pair = len(back_ref.shape) == 6

    def step(c, carry):
        rows = pl.ds(c * ROWS, ROWS)
        x = x_ref[rows, :].astype(jnp.float32)
        square = jnp.sum(x * x, axis=-1, keepdims=True) / width
        scaling = lax.rsqrt(square + epsilon)
        total = jnp.zeros((ROWS, HD), jnp.float32)
        for g in range(groups):
            for h in range(heads):
                cols = slice((g * heads + h) * HD, (g * heads + h + 1) * HD)
                grad = back_ref[g, 0, h, 0, rows, :] if pair else back_ref[g, h, 0, rows, :]
                gained = grad.astype(jnp.float32) * gain_ref[:, cols]
                total += gained * x_ref[rows, cols].astype(jnp.float32)
        mean = jnp.sum(total, axis=-1, keepdims=True) / width
        factor = scaling * scaling * scaling * mean
        for g in range(groups):
            for h in range(heads):
                cols = slice((g * heads + h) * HD, (g * heads + h + 1) * HD)
                grad = back_ref[g, 0, h, 0, rows, :] if pair else back_ref[g, h, 0, rows, :]
                gained = grad.astype(jnp.float32) * gain_ref[:, cols]
                part = scaling * gained - x_ref[rows, cols].astype(jnp.float32) * factor
                out_ref[rows, cols] = part.astype(jnp.bfloat16)
                if pair:
                    rest[0][rows, cols] = back_ref[g, 1, h, 0, rows, :]
        return carry

    lax.fori_loop(0, TILE // ROWS, step, 0)


def unnorm(x, back, gain, name):
    tokens, width = x.shape
    groups = back.shape[0]
    heads = width // HD // groups
    pair = back.ndim == 6
    outs = 2 if pair else 1
    back_block = (groups, 2, heads, 1, TILE, HD) if pair else (groups, heads, 1, TILE, HD)
    back_map = (lambda i: (0, 0, 0, i, 0, 0)) if pair else (lambda i: (0, 0, i, 0, 0))
    return pl.pallas_call(
        lambda *refs: unnorm_kernel(*refs, groups=groups, heads=heads),
        grid=(tokens // TILE,),
        out_shape=[jax.ShapeDtypeStruct((tokens, width), jnp.bfloat16)] * outs,
        in_specs=[
            pl.BlockSpec((TILE, width), lambda i: (i, 0)),
            pl.BlockSpec(back_block, back_map),
            pl.BlockSpec((1, width), lambda i: (0, 0)),
        ],
        out_specs=[pl.BlockSpec((TILE, width), lambda i: (i, 0))] * outs,
        cost_estimate=cost(12 * tokens * width, 8 * tokens * width),
        name=name,
    )(x, back, gain.reshape(1, width))


def pack_kernel(plan_ref, kv_ref, after_ref, before_ref, *, count):
    for which, out_ref in ((0, after_ref), (8, before_ref)):
        for r in range(SIDE):
            tile = plan_ref[count + which + r]
            for kv in range(2):
                out_ref[kv, 0, r] = kv_ref[tile // 2, kv, 0, tile % 2]


def pack(plan, kv, count):
    groups, _, heads, tiles, _, _ = kv.shape
    side = jax.ShapeDtypeStruct((2, heads, SIDE, TILE, HD), kv.dtype)
    side_spec = pl.BlockSpec((2, 1, SIDE, TILE, HD), lambda h: (0, h, 0, 0, 0))
    return pl.pallas_call(
        lambda *refs: pack_kernel(*refs, count=count),
        grid=(heads,),
        out_shape=[side, side],
        in_specs=[
            pl.BlockSpec(memory_space=pltpu.SMEM),
            pl.BlockSpec((groups, 2, 1, tiles, TILE, HD), lambda h: (0, 0, h, 0, 0, 0)),
        ],
        out_specs=[side_spec, side_spec],
        cost_estimate=cost(1000, 4 * kv.size),
        name="pack",
    )(plan, kv)


def merge_kernel(plan_ref, own_ref, after_ref, before_ref, out_ref, total_ref, *, count):
    total_ref[...] = own_ref[...]
    for which, side_ref in ((0, after_ref), (8, before_ref)):
        for r in range(SIDE):
            tile = plan_ref[count + which + r]
            for kv in range(2):
                total_ref[tile // 2, kv, 0, tile % 2] += side_ref[kv, 0, r].astype(jnp.float32)
    out_ref[...] = total_ref[...].astype(jnp.bfloat16)


def merge(plan, own, after, before, count):
    groups, _, heads, tiles, _, _ = own.shape
    side_spec = pl.BlockSpec((2, 1, SIDE, TILE, HD), lambda h: (0, h, 0, 0, 0))
    block = pl.BlockSpec((groups, 2, 1, tiles, TILE, HD), lambda h: (0, 0, h, 0, 0, 0))
    return pl.pallas_call(
        lambda *refs: merge_kernel(*refs, count=count),
        grid=(heads,),
        out_shape=jax.ShapeDtypeStruct(own.shape, jnp.bfloat16),
        in_specs=[pl.BlockSpec(memory_space=pltpu.SMEM), block, side_spec, side_spec],
        out_specs=block,
        scratch_shapes=[pltpu.VMEM((groups, 2, 1, tiles, TILE, HD), jnp.float32)],
        cost_estimate=cost(own.size, 6 * own.size),
        name="merge",
    )(plan, own, after, before)


def dot(a, b, dims):
    return lax.dot_general(a, b, (dims, ((), ())), preferred_element_type=jnp.float32)


def attend_kernel(
    plan_ref,
    qd_ref,
    kv_ref,
    low_ref,
    high_ref,
    dq_ref,
    own_ref,
    to_low_ref,
    to_high_ref,
    gain_ref,
    keys_ref,
    values_ref,
    dk_ref,
    dv_ref,
    *,
    blocks,
    listed,
):
    scaling = HD**-0.5
    slots = blocks + 2 * SIDE
    for b in range(blocks):
        keys_ref[b] = kv_ref[b // 2, 0, 0, b % 2]
        values_ref[b] = kv_ref[b // 2, 1, 0, b % 2]
    for r in range(SIDE):
        keys_ref[blocks + r] = low_ref[0, 0, r]
        values_ref[blocks + r] = low_ref[1, 0, r]
        keys_ref[blocks + SIDE + r] = high_ref[0, 0, r]
        values_ref[blocks + SIDE + r] = high_ref[1, 0, r]
    dk_ref[...] = jnp.zeros_like(dk_ref)
    dv_ref[...] = jnp.zeros_like(dv_ref)

    def together(first, gain_sum):
        tiles = range(GROUP)
        at = [[plan_ref[(first + t) * listed + j] for j in range(listed)] for t in tiles]
        where = [((first + t) // 2, (first + t) % 2) for t in tiles]
        queries = [qd_ref[source, 0, 0, half] for source, half in where]
        gradient = [qd_ref[source, 1, 0, half] for source, half in where]
        keys = [jnp.concatenate([keys_ref[a] for a in at[t]], axis=0) for t in tiles]
        vals = [jnp.concatenate([values_ref[a] for a in at[t]], axis=0) for t in tiles]
        scores = [dot(keys[t], queries[t], ((1,), (1,))) for t in tiles]
        dprob = [dot(vals[t], gradient[t], ((1,), (1,))) for t in tiles]
        largest = [jnp.max(x, axis=0, keepdims=True) for x in scores]
        powers = [jnp.exp((scores[t] - largest[t]) * scaling) for t in tiles]
        inverse = [1.0 / jnp.sum(x, axis=0, keepdims=True) for x in powers]
        weights = [powers[t] * inverse[t] for t in tiles]
        rounded = [x.astype(jnp.bfloat16) for x in weights]
        grad_value = [dot(rounded[t], gradient[t], ((1,), (0,))) for t in tiles]
        delta = [
            jnp.sum(rounded[t].astype(jnp.float32) * dprob[t], axis=0, keepdims=True)
            for t in tiles
        ]
        dscore = [(weights[t] * (dprob[t] - delta[t])).astype(jnp.bfloat16) for t in tiles]
        grad_key = [dot(dscore[t], queries[t], ((1,), (0,))) for t in tiles]
        grad_query = [
            (dot(dscore[t], keys[t], ((0,), (0,))) * scaling).astype(jnp.bfloat16) for t in tiles
        ]
        for t in tiles:
            dq_ref[where[t][0], 0, where[t][1]] = grad_query[t]
            product = grad_query[t].astype(jnp.float32) * queries[t].astype(jnp.float32)
            gain_sum += jnp.sum(product.reshape(-1, 8, HD), axis=0)
            for j, a in enumerate(at[t]):
                dk_ref[a] += grad_key[t][j * TILE : (j + 1) * TILE]
                dv_ref[a] += grad_value[t][j * TILE : (j + 1) * TILE]
        return gain_sum

    gain_query = jnp.zeros((8, HD), jnp.float32)
    for first in range(0, blocks, GROUP):
        gain_query = together(first, gain_query)
    gain_key = jnp.zeros((8, HD), jnp.float32)
    for s in range(slots):
        grad_key = dk_ref[s] * scaling
        gain_key += jnp.sum(
            (grad_key * keys_ref[s].astype(jnp.float32)).reshape(-1, 8, HD), axis=0
        )
        if s < blocks:
            own_ref[s // 2, 0, 0, s % 2] = grad_key
            own_ref[s // 2, 1, 0, s % 2] = dv_ref[s]
        else:
            out_ref = to_low_ref if s < blocks + SIDE else to_high_ref
            r = (s - blocks) % SIDE
            out_ref[0, 0, r] = grad_key.astype(jnp.bfloat16)
            out_ref[1, 0, r] = dv_ref[s].astype(jnp.bfloat16)
    gain_ref[0, 0:1] = jnp.sum(gain_query, axis=0, keepdims=True)
    gain_ref[0, 1:2] = jnp.sum(gain_key, axis=0, keepdims=True)


def attend(plan, qd, kv, low, high, blocks, listed):
    groups, _, heads, tiles, _, _ = kv.shape
    slots = blocks + 2 * SIDE
    side = jax.ShapeDtypeStruct(low.shape, jnp.bfloat16)
    side_spec = pl.BlockSpec((2, 1, SIDE, TILE, HD), lambda h: (0, h, 0, 0, 0))
    block = pl.BlockSpec((groups, 2, 1, tiles, TILE, HD), lambda h: (0, 0, h, 0, 0, 0))
    work = heads * blocks * TILE * listed * TILE
    return pl.pallas_call(
        lambda *refs: attend_kernel(*refs, blocks=blocks, listed=listed),
        grid=(heads,),
        out_shape=[
            jax.ShapeDtypeStruct((groups, heads, tiles, TILE, HD), jnp.bfloat16),
            jax.ShapeDtypeStruct(kv.shape, jnp.float32),
            side,
            side,
            jax.ShapeDtypeStruct((heads, 2, HD), jnp.float32),
        ],
        in_specs=[pl.BlockSpec(memory_space=pltpu.SMEM), block, block, side_spec, side_spec],
        out_specs=[
            pl.BlockSpec((groups, 1, tiles, TILE, HD), lambda h: (0, h, 0, 0, 0)),
            block,
            side_spec,
            side_spec,
            pl.BlockSpec((1, 2, HD), lambda h: (h, 0, 0)),
        ],
        scratch_shapes=[
            pltpu.VMEM((slots, TILE, HD), jnp.bfloat16),
            pltpu.VMEM((slots, TILE, HD), jnp.bfloat16),
            pltpu.VMEM((slots, TILE, HD), jnp.float32),
            pltpu.VMEM((slots, TILE, HD), jnp.float32),
        ],
        cost_estimate=cost(12 * work * HD, 20 * kv.size, work),
        name="attend",
    )(plan, qd, kv, low, high)


def swap(block):
    return lax.all_to_all(block, "head", split_axis=0, concat_axis=0, tiled=True)


def shift(block, distance):
    devices = range(lax.axis_size("ctx"))
    route = [(i - distance, i) for i in devices if i - distance in devices]
    return lax.ppermute(block, "ctx", route)


def gathered(block, axis):
    count = lax.axis_size(axis)
    copies = jnp.broadcast_to(block[None], (count,) + block.shape)
    return lax.all_to_all(copies, axis, split_axis=0, concat_axis=0, tiled=True)


def per_device(x_query, x_key, values, grad_out, gain_query, gain_key, key_tiles):
    groups = lax.axis_size("head")
    blocks = groups * x_query.shape[1] // TILE
    listed = key_tiles.shape[2]
    count = blocks * listed
    kv = swap(norm_pack(x_key[0], values[0], gain_key, groups, "norm_key"))
    plan = make_plan(key_tiles, blocks)
    qd = swap(norm_pack(x_query[0], grad_out[0], gain_query, groups, "norm_query"))
    after, before = pack(plan, kv, count)
    low, high = shift(after, 1), shift(before, -1)
    dq, own, to_low, to_high, gains = attend(plan, qd, kv, low, high, blocks, listed)
    back_query = swap(dq)
    from_after, from_before = shift(to_low, -1), shift(to_high, 1)
    merged = merge(plan, own, from_after, from_before, count)
    back = swap(merged)
    (grad_x_query,) = unnorm(x_query[0], back_query, gain_query, "unnorm_query")
    grad_x_key, grad_values = unnorm(x_key[0], back, gain_key, "unnorm_key")
    gains = jnp.sum(gathered(gains, "dp"), axis=0)
    gains = jnp.sum(gathered(gains, "ctx"), axis=0)
    gains = gathered(gains, "head").transpose(2, 0, 1, 3).reshape(2, -1)
    samples = lax.axis_size("dp")
    return (
        grad_x_query[None],
        grad_x_key[None],
        grad_values[None],
        gains[0] / gain_query / samples,
        gains[1] / gain_key / samples,
    )


def solution(mesh):
    placed = P("dp", ("ctx", "head"), None)
    return jax.shard_map(
        per_device,
        mesh=mesh,
        in_specs=(placed, placed, placed, placed, P(), P(), P("dp", None, None)),
        out_specs=(placed, placed, placed, P(), P()),
        check_vma=False,
    )
```

profile of v0, /device:TPU:24, one launch (start us, length us, event | category | flops | bytes accessed | tf_op | source)
XLA Modules:
  0.0 150.4 jit_solution(3814720235423836661)
XLA Ops:
  0.6 1.3 reshape.33.refs_2_
  1.9 3.0 %norm_key.1 = bf16[4,2,5,2,64,128]{5,4,3,2,1,0:T(8,128)(2,1)} custom-call(bf16[128,2560]{1,0:T(8,128)(2,1)} %bitcast.13, bf16[128,2560]{1,0:T(8,128)(2,1)} %bitcast.16, f32[1,2560]{1,0:T(1,128)} %reshape.33.refs_2_), custom_call_target="tpu_custom_call" | custom-call | flops 2621440 | bytes 2621440 | tf_op jit(solution)/shard_map/norm_key/pallas_call | solution.py:96
  4.9 4.4 %all-to-all-start.1 = ((bf16[4,2,5,2,64,128]{5,4,3,2,1,0:T(8,128)(2,1)}), bf16[4,2,5,2,64,128]{5,4,3,2,1,0:T(8,128)(2,1)S(1)}, u32[]{:S(2)}, u32[]{:S(2)}) async-start(bf16[4,2,5,2,64,128]{5,4,3,2,1,0:T(8,128)(2,1)} %norm_key.1), calls=%async_computation.1 | async-start | bytes 2621440 | tf_op jit(solution)/shard_map/all_to_all | solution.py:348
  10.0 3.0 %norm_query.1 = bf16[4,2,5,2,64,128]{5,4,3,2,1,0:T(8,128)(2,1)} custom-call(bf16[128,2560]{1,0:T(8,128)(2,1)} %bitcast.11, bf16[128,2560]{1,0:T(8,128)(2,1)} %bitcast.17, f32[1,2560]{1,0:T(1,128)} %reshape.32.refs_2_), custom_call_target="tpu_custom_call" | custom-call | flops 2621440 | bytes 2621440 | tf_op jit(solution)/shard_map/norm_query/pallas_call | solution.py:96
  12.9 14.3 %all-to-all-done.1.refs_1_.refs_2_ = bf16[4,2,5,2,64,128]{5,4,3,2,1,0:T(8,128)(2,1)S(1)} async-done(((bf16[4,2,5,2,64,128]{5,4,3,2,1,0:T(8,128)(2,1)}), bf16[4,2,5,2,64,128]{5,4,3,2,1,0:T(8,128)(2,1)S(1)}, u32[]{:S(2)}, u32[]{:S(2)}) %all-to-all-start.1) | async-done | bytes 1310752 | tf_op jit(solution)/shard_map/all_to_all | solution.py:348
  27.3 3.5 %all-to-all-start = ((bf16[4,2,5,2,64,128]{5,4,3,2,1,0:T(8,128)(2,1)}), bf16[4,2,5,2,64,128]{5,4,3,2,1,0:T(8,128)(2,1)S(1)}, u32[]{:S(2)}, u32[]{:S(2)}) async-start(bf16[4,2,5,2,64,128]{5,4,3,2,1,0:T(8,128)(2,1)} %norm_query.1), calls=%async_computation | async-start | bytes 2621440 | tf_op jit(solution)/shard_map/all_to_all | solution.py:348
  31.7 3.0 %plan.1.refs_0_ = s32[64]{0:T(128)} custom-call(s32[144]{0:T(256)} %reshape.31.a), custom_call_target="tpu_custom_call" | custom-call | flops 1000 | bytes 1000 | tf_op jit(solution)/shard_map/plan/pallas_call | solution.py:63
  34.7 4.1 %pack.1 = (bf16[2,5,4,64,128]{4,3,2,1,0:T(8,128)(2,1)}, bf16[2,5,4,64,128]{4,3,2,1,0:T(8,128)(2,1)}) custom-call(s32[64]{0:T(128)} %plan.1.refs_0_, bf16[4,2,5,2,64,128]{5,4,3,2,1,0:T(8,128)(2,1)} %copy-done), custom_call_target="tpu_custom_call" | custom-call | flops 1000 | bytes 2621440 | tf_op jit(solution)/shard_map/pack/pallas_call | solution.py:180
  38.8 1.9 %collective-permute-start = (bf16[2,5,4,64,128]{4,3,2,1,0:T(8,128)(2,1)}, bf16[2,5,4,64,128]{4,3,2,1,0:T(8,128)(2,1)S(1)}, u32[]{:S(2)}, u32[]{:S(2)}) collective-permute-start(bf16[2,5,4,64,128]{4,3,2,1,0:T(8,128)(2,1)} %get-tuple-element.14), channel_id=1, source_target_pairs={{0,32},{32,64},{64,96},{96,128},{128,160},{160,192},{192,224},{224... | collective-permute-start | bytes 1966088 | tf_op jit(solution)/shard_map/ppermute | solution.py:354
  40.7 3.6 %collective-permute-start.1 = (bf16[2,5,4,64,128]{4,3,2,1,0:T(8,128)(2,1)}, bf16[2,5,4,64,128]{4,3,2,1,0:T(8,128)(2,1)S(1)}, u32[]{:S(2)}, u32[]{:S(2)}) collective-permute-start(bf16[2,5,4,64,128]{4,3,2,1,0:T(8,128)(2,1)} %get-tuple-element.15), channel_id=1, source_target_pairs={{32,0},{64,32},{96,64},{128,96},{160,128},{192,160},{224,192},{256... | collective-permute-start | bytes 1966088 | tf_op jit(solution)/shard_map/ppermute | solution.py:354
  44.4 3.4 %all-to-all-done.refs_1_ = bf16[4,2,5,2,64,128]{5,4,3,2,1,0:T(8,128)(2,1)S(1)} async-done(((bf16[4,2,5,2,64,128]{5,4,3,2,1,0:T(8,128)(2,1)}), bf16[4,2,5,2,64,128]{5,4,3,2,1,0:T(8,128)(2,1)S(1)}, u32[]{:S(2)}, u32[]{:S(2)}) %all-to-all-start) | async-done | bytes 1310752 | tf_op jit(solution)/shard_map/all_to_all | solution.py:348
  47.8 3.1 %collective-permute-done.refs_3_ = bf16[2,5,4,64,128]{4,3,2,1,0:T(8,128)(2,1)S(1)} collective-permute-done((bf16[2,5,4,64,128]{4,3,2,1,0:T(8,128)(2,1)}, bf16[2,5,4,64,128]{4,3,2,1,0:T(8,128)(2,1)S(1)}, u32[]{:S(2)}, u32[]{:S(2)}) %collective-permute-start) | collective-permute-done | bytes 655392 | tf_op jit(solution)/shard_map/ppermute | solution.py:354
  50.9 1.9 %collective-permute-done.1.refs_4_ = bf16[2,5,4,64,128]{4,3,2,1,0:T(8,128)(2,1)S(1)} collective-permute-done((bf16[2,5,4,64,128]{4,3,2,1,0:T(8,128)(2,1)}, bf16[2,5,4,64,128]{4,3,2,1,0:T(8,128)(2,1)S(1)}, u32[]{:S(2)}, u32[]{:S(2)}) %collective-permute-start.1) | collective-permute-done | bytes 655392 | tf_op jit(solution)/shard_map/ppermute | solution.py:354
  52.8 0.8 copy-done.10
  53.6 12.0 %attend.1 = (bf16[4,5,2,64,128]{4,3,2,1,0:T(8,128)(2,1)}, f32[4,2,5,2,64,128]{5,4,3,2,1,0:T(8,128)}, bf16[2,5,4,64,128]{4,3,2,1,0:T(8,128)(2,1)}, bf16[2,5,4,64,128]{4,3,2,1,0:T(8,128)(2,1)}, f32[5,2,128]{2,1,0:T(2,128)}) custom-call(s32[64]{0:T(128)} %plan.1.refs_0_, bf16[4,2,5,2,64,128]{5,4,3,2,1,0:T(8,128)(2,1)} %copy-done.3, ...), custom_call_target="tpu_custom_call" | custom-call | flops 1509949440 | bytes 13107200 | tf_op jit(solution)/shard_map/attend/pallas_call | solution.py:318
  65.6 0.7 broadcast_in_dim.30
  66.3 18.2 %all_to_all.35 = f32[8,5,2,128]{3,2,1,0:T(2,128)S(1)} all-to-all(f32[8,5,2,128]{3,2,1,0:T(2,128)S(1)} %broadcast_in_dim.30), channel_id=1, replica_groups=mesh['ctx'=16,'head'=4,'dp'=8] {'dp'}, dimensions={0} | all-to-all | bytes 81920 | tf_op jit(solution)/shard_map/all_to_all | solution.py:360
  85.2 8.5 %all-to-all-start.5 = ((f32[16,5,2,128]{3,2,1,0:T(2,128)}), f32[16,5,2,128]{3,2,1,0:T(2,128)S(1)}, u32[]{:S(2)}, u32[]{:S(2)}) async-start(f32[16,5,2,128]{3,2,1,0:T(2,128)} %broadcast_in_dim.31), calls=%async_computation.5 | async-start | bytes 163840 | tf_op jit(solution)/shard_map/all_to_all | solution.py:360
  93.8 2.2 %collective-permute-start.2 = (bf16[2,5,4,64,128]{4,3,2,1,0:T(8,128)(2,1)}, bf16[2,5,4,64,128]{4,3,2,1,0:T(8,128)(2,1)S(1)}, u32[]{:S(2)}, u32[]{:S(2)}) collective-permute-start(bf16[2,5,4,64,128]{4,3,2,1,0:T(8,128)(2,1)} %get-tuple-element.18), channel_id=1, source_target_pairs={{32,0},{64,32},{96,64},{128,96},{160,128},{192,160},{224,192},{256... | collective-permute-start | bytes 1966088 | tf_op jit(solution)/shard_map/ppermute | solution.py:354
  96.0 2.1 %collective-permute-start.3 = (bf16[2,5,4,64,128]{4,3,2,1,0:T(8,128)(2,1)}, bf16[2,5,4,64,128]{4,3,2,1,0:T(8,128)(2,1)S(1)}, u32[]{:S(2)}, u32[]{:S(2)}) collective-permute-start(bf16[2,5,4,64,128]{4,3,2,1,0:T(8,128)(2,1)} %get-tuple-element.19), channel_id=1, source_target_pairs={{0,32},{32,64},{64,96},{96,128},{128,160},{160,192},{192,224},{224... | collective-permute-start | bytes 1966088 | tf_op jit(solution)/shard_map/ppermute | solution.py:354
  98.1 0.9 all-to-all-done.5
  99.0 9.9 %all_to_all.36 = f32[4,5,2,128]{3,2,1,0:T(2,128)S(1)} all-to-all(f32[4,5,2,128]{3,2,1,0:T(2,128)S(1)} %broadcast_in_dim.32), channel_id=1, replica_groups=mesh['ctx'=16,'head'=4,'dp'=8] {'head'}, dimensions={0} | all-to-all | bytes 40960 | tf_op jit(solution)/shard_map/all_to_all | solution.py:360
  109.0 3.5 %all-to-all-start.2 = ((bf16[4,5,2,64,128]{4,3,2,1,0:T(8,128)(2,1)}), bf16[4,5,2,64,128]{4,3,2,1,0:T(8,128)(2,1)S(1)}, u32[]{:S(2)}, u32[]{:S(2)}) async-start(bf16[4,5,2,64,128]{4,3,2,1,0:T(8,128)(2,1)} %get-tuple-element.16), calls=%async_computation.2 | async-start | bytes 1310720 | tf_op jit(solution)/shard_map/all_to_all | solution.py:348
  112.5 0.8 copy-done.4
  113.5 4.8 %merge.1 = bf16[4,2,5,2,64,128]{5,4,3,2,1,0:T(8,128)(2,1)} custom-call(s32[64]{0:T(128)} %plan.1.refs_0_, f32[4,2,5,2,64,128]{5,4,3,2,1,0:T(8,128)} %get-tuple-element.17.refs_1_, bf16[2,5,4,64,128]{4,3,2,1,0:T(8,128)(2,1)} %copy-done.4, bf16[2,5,4,64,128]{4,3,2,1,0:T(8,128)(2,1)} %copy-done.5), custom_call_target="tpu_custom_call" | custom-call | flops 655360 | bytes 3932160 | tf_op jit(solution)/shard_map/merge/pallas_call | solution.py:208
  118.4 5.6 %all-to-all-done.2.refs_1_ = bf16[4,5,2,64,128]{4,3,2,1,0:T(8,128)(2,1)S(1)} async-done(((bf16[4,5,2,64,128]{4,3,2,1,0:T(8,128)(2,1)}), bf16[4,5,2,64,128]{4,3,2,1,0:T(8,128)(2,1)S(1)}, u32[]{:S(2)}, u32[]{:S(2)}) %all-to-all-start.2) | async-done | bytes 655392 | tf_op jit(solution)/shard_map/all_to_all | solution.py:348
  124.0 0.8 copy-done.2
  124.9 3.5 %all-to-all-start.3 = ((bf16[4,2,5,2,64,128]{5,4,3,2,1,0:T(8,128)(2,1)}), bf16[4,2,5,2,64,128]{5,4,3,2,1,0:T(8,128)(2,1)S(1)}, u32[]{:S(2)}, u32[]{:S(2)}) async-start(bf16[4,2,5,2,64,128]{5,4,3,2,1,0:T(8,128)(2,1)} %merge.1), calls=%async_computation.3 | async-start | bytes 2621440 | tf_op jit(solution)/shard_map/all_to_all | solution.py:348
  129.1 3.0 %unnorm_query.1 = bf16[128,2560]{1,0:T(8,128)(2,1)} custom-call(bf16[128,2560]{1,0:T(8,128)(2,1)} %bitcast.12, bf16[4,5,2,64,128]{4,3,2,1,0:T(8,128)(2,1)} %copy-done.2, f32[1,2560]{1,0:T(1,128)} %reshape.32.refs_2_), custom_call_target="tpu_custom_call" | custom-call | flops 3932160 | bytes 2621440 | tf_op jit(solution)/shard_map/unnorm_query/pallas_call | solution.py:153
  132.1 14.0 %all-to-all-done.3.refs_1_ = bf16[4,2,5,2,64,128]{5,4,3,2,1,0:T(8,128)(2,1)S(1)} async-done(((bf16[4,2,5,2,64,128]{5,4,3,2,1,0:T(8,128)(2,1)}), bf16[4,2,5,2,64,128]{5,4,3,2,1,0:T(8,128)(2,1)S(1)}, u32[]{:S(2)}, u32[]{:S(2)}) %all-to-all-start.3) | async-done | bytes 1310752 | tf_op jit(solution)/shard_map/all_to_all | solution.py:348
  146.1 1.1 copy-done.1
  147.2 3.2 %unnorm_key.1 = (bf16[128,2560]{1,0:T(8,128)(2,1)}, bf16[128,2560]{1,0:T(8,128)(2,1)}) custom-call(bf16[128,2560]{1,0:T(8,128)(2,1)} %bitcast.14, bf16[4,2,5,2,64,128]{5,4,3,2,1,0:T(8,128)(2,1)} %copy-done.1, f32[1,2560]{1,0:T(1,128)} %reshape.33.refs_2_), custom_call_target="tpu_custom_call" | custom-call | flops 3932160 | bytes 2621440 | tf_op jit(solution)/shard_map/unnorm_key/pallas_call | solution.py:153
  (34 shorter events, 3.1 us)
Async XLA Ops:
  4.9 4.4 %copy-start.6 = (f32[2560]{0:T(1024)S(1)}, f32[2560]{0:T(1024)}, u32[]{:S(2)}) copy-start(f32[2560]{0:T(1024)} %param.11) | copy-start | bytes 30724
  4.9 22.3 %all-to-all-start.1 = ((bf16[4,2,5,2,64,128]{5,4,3,2,1,0:T(8,128)(2,1)}), bf16[4,2,5,2,64,128]{5,4,3,2,1,0:T(8,128)(2,1)S(1)}, u32[]{:S(2)}, u32[]{:S(2)}) async-start(bf16[4,2,5,2,64,128]{5,4,3,2,1,0:T(8,128)(2,1)} %norm_key.1), calls=%async_computation.1 | async-start | bytes 2621440 | tf_op jit(solution)/shard_map/all_to_all | solution.py:348
  12.9 17.9 %copy-start.8 = (s32[1,128,6]{1,0,2:T(1,128)S(1)}, s32[1,128,6]{1,0,2:T(1,128)}, u32[]{:S(2)}) copy-start(s32[1,128,6]{1,0,2:T(1,128)} %param.13) | copy-start | bytes 9220
  27.2 3.6 %copy-start = (bf16[4,2,5,2,64,128]{5,4,3,2,1,0:T(8,128)(2,1)}, bf16[4,2,5,2,64,128]{5,4,3,2,1,0:T(8,128)(2,1)S(1)}, u32[]{:S(2)}) copy-start(bf16[4,2,5,2,64,128]{5,4,3,2,1,0:T(8,128)(2,1)S(1)} %all-to-all-done.1.refs_1_.refs_2_) | copy-start | bytes 3932164
  27.3 20.6 %all-to-all-start = ((bf16[4,2,5,2,64,128]{5,4,3,2,1,0:T(8,128)(2,1)}), bf16[4,2,5,2,64,128]{5,4,3,2,1,0:T(8,128)(2,1)S(1)}, u32[]{:S(2)}, u32[]{:S(2)}) async-start(bf16[4,2,5,2,64,128]{5,4,3,2,1,0:T(8,128)(2,1)} %norm_query.1), calls=%async_computation | async-start | bytes 2621440 | tf_op jit(solution)/shard_map/all_to_all | solution.py:348
  38.8 12.1 %collective-permute-start = (bf16[2,5,4,64,128]{4,3,2,1,0:T(8,128)(2,1)}, bf16[2,5,4,64,128]{4,3,2,1,0:T(8,128)(2,1)S(1)}, u32[]{:S(2)}, u32[]{:S(2)}) collective-permute-start(bf16[2,5,4,64,128]{4,3,2,1,0:T(8,128)(2,1)} %get-tuple-element.14), channel_id=1, source_target_pairs={{0,32},{32,64},{64,96},{96,128},{128,160},{160,192},{192,224},{224... | collective-permute-start | bytes 1966088 | tf_op jit(solution)/shard_map/ppermute | solution.py:354
  40.7 12.0 %collective-permute-start.1 = (bf16[2,5,4,64,128]{4,3,2,1,0:T(8,128)(2,1)}, bf16[2,5,4,64,128]{4,3,2,1,0:T(8,128)(2,1)S(1)}, u32[]{:S(2)}, u32[]{:S(2)}) collective-permute-start(bf16[2,5,4,64,128]{4,3,2,1,0:T(8,128)(2,1)} %get-tuple-element.15), channel_id=1, source_target_pairs={{32,0},{64,32},{96,64},{128,96},{160,128},{192,160},{224,192},{256... | collective-permute-start | bytes 1966088 | tf_op jit(solution)/shard_map/ppermute | solution.py:354
  47.8 5.0 %copy-start.3 = (bf16[4,2,5,2,64,128]{5,4,3,2,1,0:T(8,128)(2,1)}, bf16[4,2,5,2,64,128]{5,4,3,2,1,0:T(8,128)(2,1)S(1)}, u32[]{:S(2)}) copy-start(bf16[4,2,5,2,64,128]{5,4,3,2,1,0:T(8,128)(2,1)S(1)} %all-to-all-done.refs_1_) | copy-start | bytes 3932164
  50.9 1.9 %copy-start.9 = (bf16[2,5,4,64,128]{4,3,2,1,0:T(8,128)(2,1)}, bf16[2,5,4,64,128]{4,3,2,1,0:T(8,128)(2,1)S(1)}, u32[]{:S(2)}) copy-start(bf16[2,5,4,64,128]{4,3,2,1,0:T(8,128)(2,1)S(1)} %collective-permute-done.refs_3_) | copy-start | bytes 1966084
  52.8 0.8 copy-start.10
  85.2 13.7 %all-to-all-start.5 = ((f32[16,5,2,128]{3,2,1,0:T(2,128)}), f32[16,5,2,128]{3,2,1,0:T(2,128)S(1)}, u32[]{:S(2)}, u32[]{:S(2)}) async-start(f32[16,5,2,128]{3,2,1,0:T(2,128)} %broadcast_in_dim.31), calls=%async_computation.5 | async-start | bytes 163840 | tf_op jit(solution)/shard_map/all_to_all | solution.py:360
  93.8 18.7 %collective-permute-start.2 = (bf16[2,5,4,64,128]{4,3,2,1,0:T(8,128)(2,1)}, bf16[2,5,4,64,128]{4,3,2,1,0:T(8,128)(2,1)S(1)}, u32[]{:S(2)}, u32[]{:S(2)}) collective-permute-start(bf16[2,5,4,64,128]{4,3,2,1,0:T(8,128)(2,1)} %get-tuple-element.18), channel_id=1, source_target_pairs={{32,0},{64,32},{96,64},{128,96},{160,128},{192,160},{224,192},{256... | collective-permute-start | bytes 1966088 | tf_op jit(solution)/shard_map/ppermute | solution.py:354
  96.0 16.5 %collective-permute-start.3 = (bf16[2,5,4,64,128]{4,3,2,1,0:T(8,128)(2,1)}, bf16[2,5,4,64,128]{4,3,2,1,0:T(8,128)(2,1)S(1)}, u32[]{:S(2)}, u32[]{:S(2)}) collective-permute-start(bf16[2,5,4,64,128]{4,3,2,1,0:T(8,128)(2,1)} %get-tuple-element.19), channel_id=1, source_target_pairs={{0,32},{32,64},{64,96},{96,128},{128,160},{160,192},{192,224},{224... | collective-permute-start | bytes 1966088 | tf_op jit(solution)/shard_map/ppermute | solution.py:354
  109.0 15.0 %all-to-all-start.2 = ((bf16[4,5,2,64,128]{4,3,2,1,0:T(8,128)(2,1)}), bf16[4,5,2,64,128]{4,3,2,1,0:T(8,128)(2,1)S(1)}, u32[]{:S(2)}, u32[]{:S(2)}) async-start(bf16[4,5,2,64,128]{4,3,2,1,0:T(8,128)(2,1)} %get-tuple-element.16), calls=%async_computation.2 | async-start | bytes 1310720 | tf_op jit(solution)/shard_map/all_to_all | solution.py:348
  112.5 0.8 copy-start.4
  112.5 1.0 copy-start.5
  118.4 10.1 %copy-start.7 = (f32[2560]{0:T(1024)S(1)}, f32[2560]{0:T(1024)}, u32[]{:S(2)}) copy-start(f32[2560]{0:T(1024)} %param.12) | copy-start | bytes 30724
  124.0 0.8 copy-start.2
  124.9 21.3 %all-to-all-start.3 = ((bf16[4,2,5,2,64,128]{5,4,3,2,1,0:T(8,128)(2,1)}), bf16[4,2,5,2,64,128]{5,4,3,2,1,0:T(8,128)(2,1)S(1)}, u32[]{:S(2)}, u32[]{:S(2)}) async-start(bf16[4,2,5,2,64,128]{5,4,3,2,1,0:T(8,128)(2,1)} %merge.1), calls=%async_computation.3 | async-start | bytes 2621440 | tf_op jit(solution)/shard_map/all_to_all | solution.py:348
  146.1 1.1 copy-start.1
where the time goes:
time: 151 us; the launch traced here: 150 us
  waiting for transfers between devices  43.3 us (29%)
  Pallas kernels  36.1 us (24%)
  starting transfers between devices  33.4 us (22%)
  blocking collectives  28.2 us (19%)
  local copies, waits for them, and re-layouts  7.99 us (5%)
    all_to_all x4, waiting for transfers between devices, swap(): lax.all_to_all(block, 'head', split_axis=0, concat_axis=0, tiled=True)  37.4 us
    all_to_all x2, blocking collectives, gathered(): return lax.all_to_all(copies, axis, split_axis=0, concat_axis=0, tiled=True)  28.2 us
    all_to_all x4, starting transfers between devices, swap(): lax.all_to_all(block, 'head', split_axis=0, concat_axis=0, tiled=True)  15 us
    pallas_call x1, Pallas kernels, attend(): pl.pallas_call(lambda *refs: attend_kernel(*refs, blocks=blocks, listed=l...  12 us
    ppermute x4, starting transfers between devices, shift(): return lax.ppermute(block, 'ctx', route)  9.86 us
    all_to_all x1, starting transfers between devices, gathered(): return lax.all_to_all(copies, axis, split_axis=0, concat_axis=0, tiled=True)  8.53 us
    pallas_call x2, Pallas kernels, unnorm(): pl.pallas_call(lambda *refs: unnorm_kernel(*refs, groups=groups, heads=he...  6.18 us
    pallas_call x2, Pallas kernels, norm_pack(): pl.pallas_call(lambda *refs: norm_kernel(*refs, groups=groups, heads=head...  5.96 us
  transfers between devices with their start and end apart: 9, of which 7 were waited for; matrix products, arithmetic and copies ran while one was open for 1% of the time, Pallas kernels for 12%

commit v1 on v0

--- a/solution.py
+++ b/solution.py
@@ -17,6 +17,14 @@
 
 def cost(flops, moved, exps=0):
     return pl.CostEstimate(flops=flops, bytes_accessed=moved, transcendentals=exps)
+
+
+def room(mebibytes):
+    return pltpu.CompilerParams(vmem_limit_bytes=mebibytes << 20)
+
+
+def in_hbm(block):
+    return pltpu.with_memory_space_constraint(block, pltpu.HBM)
 
 
 def plan_kernel(listed_ref, plan_ref, slot_ref, *, blocks, listed):
@@ -81,7 +89,7 @@
         for g in range(groups):
             for h in range(heads):
                 cols = slice((g * heads + h) * HD, (g * heads + h + 1) * HD)
-                part = x_ref[rows, cols].astype(jnp.float32) * scaling * gain_ref[:, cols]
+                part = x_ref[rows, cols].astype(jnp.float32) * scaling * gain_ref[cols][None, :]
                 out_ref[g, 0, h, 0, rows, :] = part.astype(jnp.bfloat16)
                 out_ref[g, 1, h, 0, rows, :] = y_ref[rows, cols]
         return carry
@@ -89,7 +97,7 @@
     lax.fori_loop(0, TILE // ROWS, step, 0)
 
 
-def norm_pack(x, y, gain, groups, name):
+def norm_pack(x, y, gain, groups, name, grant):
     tokens, width = x.shape
     heads = width // HD // groups
     tiles = tokens // TILE
@@ -100,69 +108,66 @@
         in_specs=[
             pl.BlockSpec((TILE, width), lambda i: (i, 0)),
             pl.BlockSpec((TILE, width), lambda i: (i, 0)),
-            pl.BlockSpec((1, width), lambda i: (0, 0)),
+            pl.BlockSpec((width,), lambda i: (0,)),
         ],
         out_specs=pl.BlockSpec(
             (groups, 2, heads, 1, TILE, HD), lambda i: (0, 0, 0, i, 0, 0)
         ),
+        compiler_params=room(grant),
         cost_estimate=cost(8 * tokens * width, 8 * tokens * width),
         name=name,
-    )(x, y, gain.reshape(1, width))
-
-
-def unnorm_kernel(x_ref, back_ref, gain_ref, out_ref, *rest, groups, heads):
+    )(x, y, gain)
+
+
+def unnorm_kernel(xq_ref, xk_ref, back_ref, gq_ref, gk_ref, oq_ref, ok_ref, ov_ref, *, groups, heads):
     width = groups * heads * HD
-    pair = len(back_ref.shape) == 6
+    places = [(g, h, slice((g * heads + h) * HD, (g * heads + h + 1) * HD)) for g in range(groups) for h in range(heads)]
 
     def step(c, carry):
         rows = pl.ds(c * ROWS, ROWS)
-        x = x_ref[rows, :].astype(jnp.float32)
-        square = jnp.sum(x * x, axis=-1, keepdims=True) / width
-        scaling = lax.rsqrt(square + epsilon)
-        total = jnp.zeros((ROWS, HD), jnp.float32)
-        for g in range(groups):
-            for h in range(heads):
-                cols = slice((g * heads + h) * HD, (g * heads + h + 1) * HD)
-                grad = back_ref[g, 0, h, 0, rows, :] if pair else back_ref[g, h, 0, rows, :]
-                gained = grad.astype(jnp.float32) * gain_ref[:, cols]
-                total += gained * x_ref[rows, cols].astype(jnp.float32)
-        mean = jnp.sum(total, axis=-1, keepdims=True) / width
-        factor = scaling * scaling * scaling * mean
-        for g in range(groups):
-            for h in range(heads):
-                cols = slice((g * heads + h) * HD, (g * heads + h + 1) * HD)
-                grad = back_ref[g, 0, h, 0, rows, :] if pair else back_ref[g, h, 0, rows, :]
-                gained = grad.astype(jnp.float32) * gain_ref[:, cols]
-                part = scaling * gained - x_ref[rows, cols].astype(jnp.float32) * factor
-                out_ref[rows, cols] = part.astype(jnp.bfloat16)
-                if pair:
-                    rest[0][rows, cols] = back_ref[g, 1, h, 0, rows, :]
+        for which, x_ref, gain_ref, out_ref in ((0, xq_ref, gq_ref, oq_ref), (1, xk_ref, gk_ref, ok_ref)):
+            square = jnp.zeros((ROWS, HD), jnp.float32)
+            total = jnp.zeros((ROWS, HD), jnp.float32)
+            for g, h, cols in places:
+                x = x_ref[rows, cols].astype(jnp.float32)
+                gained = back_ref[g, which, h, 0, rows, :].astype(jnp.float32) * gain_ref[cols][None, :]
+                square += x * x
+                total += gained * x
+            scaling = lax.rsqrt(jnp.sum(square, axis=-1, keepdims=True) / width + epsilon)
+            mean = jnp.sum(total, axis=-1, keepdims=True) / width
+            factor = scaling * scaling * scaling * mean
+            for g, h, cols in places:
+                x = x_ref[rows, cols].astype(jnp.float32)
+                gained = back_ref[g, which, h, 0, rows, :].astype(jnp.float32) * gain_ref[cols][None, :]
+                out_ref[rows, cols] = (scaling * gained - x * factor).astype(jnp.bfloat16)
+                if which:
+                    ov_ref[rows, cols] = back_ref[g, 2, h, 0, rows, :]
         return carry
 
     lax.fori_loop(0, TILE // ROWS, step, 0)
 
 
-def unnorm(x, back, gain, name):
-    tokens, width = x.shape
-    groups = back.shape[0]
-    heads = width // HD // groups
-    pair = back.ndim == 6
-    outs = 2 if pair else 1
-    back_block = (groups, 2, heads, 1, TILE, HD) if pair else (groups, heads, 1, TILE, HD)
-    back_map = (lambda i: (0, 0, 0, i, 0, 0)) if pair else (lambda i: (0, 0, i, 0, 0))
+def unnorm(xq, xk, back, gain_query, gain_key):
+    tokens, width = xq.shape
+    groups, _, heads = back.shape[:3]
+    rows = pl.BlockSpec((TILE, width), lambda i: (i, 0))
+    gain = pl.BlockSpec((width,), lambda i: (0,))
     return pl.pallas_call(
         lambda *refs: unnorm_kernel(*refs, groups=groups, heads=heads),
         grid=(tokens // TILE,),
-        out_shape=[jax.ShapeDtypeStruct((tokens, width), jnp.bfloat16)] * outs,
+        out_shape=[jax.ShapeDtypeStruct((tokens, width), jnp.bfloat16)] * 3,
         in_specs=[
-            pl.BlockSpec((TILE, width), lambda i: (i, 0)),
-            pl.BlockSpec(back_block, back_map),
-            pl.BlockSpec((1, width), lambda i: (0, 0)),
-        ],
-        out_specs=[pl.BlockSpec((TILE, width), lambda i: (i, 0))] * outs,
-        cost_estimate=cost(12 * tokens * width, 8 * tokens * width),
-        name=name,
-    )(x, back, gain.reshape(1, width))
+            rows,
+            rows,
+            pl.BlockSpec((groups, 3, heads, 1, TILE, HD), lambda i: (0, 0, 0, i, 0, 0)),
+            gain,
+            gain,
+        ],
+        out_specs=[rows] * 3,
+        compiler_params=room(16),
+        cost_estimate=cost(24 * tokens * width, 16 * tokens * width),
+        name="unnorm",
+    )(xq, xk, back, gain_query, gain_key)
 
 
 def pack_kernel(plan_ref, kv_ref, after_ref, before_ref, *, count):
@@ -186,35 +191,43 @@
             pl.BlockSpec((groups, 2, 1, tiles, TILE, HD), lambda h: (0, 0, h, 0, 0, 0)),
         ],
         out_specs=[side_spec, side_spec],
+        compiler_params=room(8),
         cost_estimate=cost(1000, 4 * kv.size),
         name="pack",
     )(plan, kv)
 
 
-def merge_kernel(plan_ref, own_ref, after_ref, before_ref, out_ref, total_ref, *, count):
-    total_ref[...] = own_ref[...]
+def merge_kernel(plan_ref, dq_ref, own_ref, after_ref, before_ref, out_ref, total_ref, *, count):
+    total_ref[...] = own_ref[:, :, 0].astype(jnp.float32)
     for which, side_ref in ((0, after_ref), (8, before_ref)):
         for r in range(SIDE):
             tile = plan_ref[count + which + r]
             for kv in range(2):
-                total_ref[tile // 2, kv, 0, tile % 2] += side_ref[kv, 0, r].astype(jnp.float32)
-    out_ref[...] = total_ref[...].astype(jnp.bfloat16)
-
-
-def merge(plan, own, after, before, count):
+                total_ref[tile // 2, kv, tile % 2] += side_ref[kv, 0, r].astype(jnp.float32)
+    out_ref[:, 0, 0] = dq_ref[:, 0]
+    out_ref[:, 1:, 0] = total_ref[...].astype(jnp.bfloat16)
+
+
+def merge(plan, dq, own, after, before, count):
     groups, _, heads, tiles, _, _ = own.shape
     side_spec = pl.BlockSpec((2, 1, SIDE, TILE, HD), lambda h: (0, h, 0, 0, 0))
-    block = pl.BlockSpec((groups, 2, 1, tiles, TILE, HD), lambda h: (0, 0, h, 0, 0, 0))
     return pl.pallas_call(
         lambda *refs: merge_kernel(*refs, count=count),
         grid=(heads,),
-        out_shape=jax.ShapeDtypeStruct(own.shape, jnp.bfloat16),
-        in_specs=[pl.BlockSpec(memory_space=pltpu.SMEM), block, side_spec, side_spec],
-        out_specs=block,
-        scratch_shapes=[pltpu.VMEM((groups, 2, 1, tiles, TILE, HD), jnp.float32)],
+        out_shape=jax.ShapeDtypeStruct((groups, 3, heads, tiles, TILE, HD), jnp.bfloat16),
+        in_specs=[
+            pl.BlockSpec(memory_space=pltpu.SMEM),
+            pl.BlockSpec((groups, 1, tiles, TILE, HD), lambda h: (0, h, 0, 0, 0)),
+            pl.BlockSpec((groups, 2, 1, tiles, TILE, HD), lambda h: (0, 0, h, 0, 0, 0)),
+            side_spec,
+            side_spec,
+        ],
+        out_specs=pl.BlockSpec((groups, 3, 1, tiles, TILE, HD), lambda h: (0, 0, h, 0, 0, 0)),
+        scratch_shapes=[pltpu.VMEM((groups, 2, tiles, TILE, HD), jnp.float32)],
+        compiler_params=room(8),
         cost_estimate=cost(own.size, 6 * own.size),
         name="merge",
-    )(plan, own, after, before)
+    )(plan, dq, own, after, before)
 
 
 def dot(a, b, dims):
@@ -250,6 +263,11 @@
         values_ref[blocks + r] = low_ref[1, 0, r]
         keys_ref[blocks + SIDE + r] = high_ref[0, 0, r]
         values_ref[blocks + SIDE + r] = high_ref[1, 0, r]
+
+    @pl.when(pl.program_id(0) == 0)
+    def _():
+        gain_ref[...] = jnp.zeros_like(gain_ref)
+
     dk_ref[...] = jnp.zeros_like(dk_ref)
     dv_ref[...] = jnp.zeros_like(dv_ref)
 
@@ -297,15 +315,16 @@
             (grad_key * keys_ref[s].astype(jnp.float32)).reshape(-1, 8, HD), axis=0
         )
         if s < blocks:
-            own_ref[s // 2, 0, 0, s % 2] = grad_key
-            own_ref[s // 2, 1, 0, s % 2] = dv_ref[s]
+            own_ref[s // 2, 0, 0, s % 2] = grad_key.astype(jnp.bfloat16)
+            own_ref[s // 2, 1, 0, s % 2] = dv_ref[s].astype(jnp.bfloat16)
         else:
             out_ref = to_low_ref if s < blocks + SIDE else to_high_ref
             r = (s - blocks) % SIDE
             out_ref[0, 0, r] = grad_key.astype(jnp.bfloat16)
             out_ref[1, 0, r] = dv_ref[s].astype(jnp.bfloat16)
-    gain_ref[0, 0:1] = jnp.sum(gain_query, axis=0, keepdims=True)
-    gain_ref[0, 1:2] = jnp.sum(gain_key, axis=0, keepdims=True)
+    head = pl.program_id(0)
+    for which, part in ((0, gain_query), (8, gain_key)):
+        gain_ref[pl.ds(which + head, 1)] = jnp.sum(part, axis=0, keepdims=True)
 
 
 def attend(plan, qd, kv, low, high, blocks, listed):
@@ -320,10 +339,10 @@
         grid=(heads,),
         out_shape=[
             jax.ShapeDtypeStruct((groups, heads, tiles, TILE, HD), jnp.bfloat16),
-            jax.ShapeDtypeStruct(kv.shape, jnp.float32),
+            pltpu.HBM(kv.shape, jnp.bfloat16),
             side,
             side,
-            jax.ShapeDtypeStruct((heads, 2, HD), jnp.float32),
+            jax.ShapeDtypeStruct((16, HD), jnp.float32),
         ],
         in_specs=[pl.BlockSpec(memory_space=pltpu.SMEM), block, block, side_spec, side_spec],
         out_specs=[
@@ -331,7 +350,7 @@
             block,
             side_spec,
             side_spec,
-            pl.BlockSpec((1, 2, HD), lambda h: (h, 0, 0)),
+            pl.BlockSpec((16, HD), lambda h: (0, 0)),
         ],
         scratch_shapes=[
             pltpu.VMEM((slots, TILE, HD), jnp.bfloat16),
@@ -339,6 +358,7 @@
             pltpu.VMEM((slots, TILE, HD), jnp.float32),
             pltpu.VMEM((slots, TILE, HD), jnp.float32),
         ],
+        compiler_params=room(24),
         cost_estimate=cost(12 * work * HD, 20 * kv.size, work),
         name="attend",
     )(plan, qd, kv, low, high)
@@ -365,21 +385,25 @@
     blocks = groups * x_query.shape[1] // TILE
     listed = key_tiles.shape[2]
     count = blocks * listed
-    kv = swap(norm_pack(x_key[0], values[0], gain_key, groups, "norm_key"))
-    plan = make_plan(key_tiles, blocks)
-    qd = swap(norm_pack(x_query[0], grad_out[0], gain_query, groups, "norm_query"))
+    kv = swap(norm_pack(x_key[0], values[0], gain_key, groups, "norm_key", 60))
+    plan, gain = lax.optimization_barrier((make_plan(key_tiles, blocks), gain_query))
+    qd = swap(norm_pack(x_query[0], grad_out[0], gain, groups, "norm_query", 16))
     after, before = pack(plan, kv, count)
-    low, high = shift(after, 1), shift(before, -1)
+    low, high = (in_hbm(side) for side in (shift(after, 1), shift(before, -1)))
     dq, own, to_low, to_high, gains = attend(plan, qd, kv, low, high, blocks, listed)
-    back_query = swap(dq)
     from_after, from_before = shift(to_low, -1), shift(to_high, 1)
-    merged = merge(plan, own, from_after, from_before, count)
+    gains = jnp.sum(gathered(gains, "dp"), axis=0)
+    from_after, from_before, gains = lax.optimization_barrier((from_after, from_before, gains))
+    merged = merge(plan, dq, own, from_after, from_before, count)
+    merged, gains = lax.optimization_barrier((merged, gains))
     back = swap(merged)
-    (grad_x_query,) = unnorm(x_query[0], back_query, gain_query, "unnorm_query")
-    grad_x_key, grad_values = unnorm(x_key[0], back, gain_key, "unnorm_key")
-    gains = jnp.sum(gathered(gains, "dp"), axis=0)
-    gains = jnp.sum(gathered(gains, "ctx"), axis=0)
-    gains = gathered(gains, "head").transpose(2, 0, 1, 3).reshape(2, -1)
+    gains = jnp.sum(lax.all_gather(gains, "ctx"), axis=0)
+    gains = lax.all_gather(gains, "head")
+    grad_x_query, grad_x_key, grad_values = unnorm(
+        x_query[0], x_key[0], back, gain_query, gain_key
+    )
+    heads = x_query.shape[2] // HD // groups
+    gains = [gains[:, at : at + heads].reshape(-1) for at in (0, 8)]
     samples = lax.axis_size("dp")
     return (
         grad_x_query[None],

time: 151 us -> 130 us (0.86)
  waiting for transfers between devices: 43.3 us -> 20.9 us
  blocking collectives: 28.2 us -> 49.6 us
  Pallas kernels: 36.1 us -> 27 us
  starting transfers between devices: 33.4 us -> 25.8 us
  local copies, waits for them, and re-layouts: 7.99 us -> 4.3 us
    all_gather x0 -> x2, blocking collectives: none -> 31.1 us  [the longest x1 16.1 us: per_device(): gains = jnp.sum(lax.all_gather(gains, 'ctx'), axis=0)]
    all_to_all x4 -> x3, waiting for transfers between devices: 37.4 us -> 20.8 us  [swap(): lax.all_to_all(block, 'head', split_axis=0, concat_axis=0, tiled=True)]
    all_to_all x2 -> x1, blocking collectives: 28.2 us -> 18.5 us  [gathered(): return lax.all_to_all(copies, axis, split_axis=0, concat_axis=0, tiled=True)]
    all_to_all x1 -> x0, starting transfers between devices: 8.53 us -> none  [gathered(): return lax.all_to_all(copies, axis, split_axis=0, concat_axis=0, tiled=True)]
    ppermute x4, waiting for transfers between devices: 4.98 us -> 0.01 us  [shift(): return lax.ppermute(block, 'ctx', route)]
    pallas_call x2 -> x1, Pallas kernels: 6.18 us -> 2.64 us  [unnorm(): pl.pallas_call(lambda *refs: unnorm_kernel(*refs, groups=groups, heads=he...]
    pallas_call x1, Pallas kernels: 4.84 us -> 1.63 us  [merge(): pl.pallas_call(lambda *refs: merge_kernel(*refs, count=count), grid=(head...]
    ppermute x4, starting transfers between devices: 9.86 us -> 12.3 us  [shift(): return lax.ppermute(block, 'ctx', route)]
  transfers between devices with their start and end apart: 9 -> 7, of which waited for: 7 -> 2; matrix products, arithmetic and copies ran while one was open for 1% -> 1% of each run, Pallas kernels for 12% -> 6%
where the time goes in v1:
time: 130 us; the launch traced here: 129 us
  blocking collectives  49.6 us (38%)
  Pallas kernels  27 us (21%)
  starting transfers between devices  25.8 us (20%)
  waiting for transfers between devices  20.9 us (16%)
  local copies, waits for them, and re-layouts  4.3 us (3%)
    all_to_all x3, waiting for transfers between devices, swap(): lax.all_to_all(block, 'head', split_axis=0, concat_axis=0, tiled=True)  20.8 us
    all_to_all x1, blocking collectives, gathered(): return lax.all_to_all(copies, axis, split_axis=0, concat_axis=0, tiled=True)  18.5 us
    all_gather x1, blocking collectives, per_device(): gains = jnp.sum(lax.all_gather(gains, 'ctx'), axis=0)  16.1 us
    all_gather x1, blocking collectives, per_device(): gains = lax.all_gather(gains, 'head')  15 us
    all_to_all x3, starting transfers between devices, swap(): lax.all_to_all(block, 'head', split_axis=0, concat_axis=0, tiled=True)  13.6 us
    ppermute x4, starting transfers between devices, shift(): return lax.ppermute(block, 'ctx', route)  12.3 us
    pallas_call x1, Pallas kernels, attend(): pl.pallas_call(lambda *refs: attend_kernel(*refs, blocks=blocks, listed=l...  12.1 us
    pallas_call x2, Pallas kernels, norm_pack(): pl.pallas_call(lambda *refs: norm_kernel(*refs, groups=groups, heads=head...  4.86 us
  transfers between devices with their start and end apart: 7, of which 2 were waited for; matrix products, arithmetic and copies ran while one was open for 1% of the time, Pallas kernels for 6%

profile of v1, /device:TPU:24, one launch (start us, length us, event | category | flops | bytes accessed | tf_op | source)
XLA Modules:
  0.0 129.1 jit_solution(930685618373827684)
XLA Ops:
  0.6 3.0 %norm_key.1 = bf16[4,2,5,2,64,128]{5,4,3,2,1,0:T(8,128)(2,1)} custom-call(bf16[128,2560]{1,0:T(8,128)(2,1)} %bitcast.14, bf16[128,2560]{1,0:T(8,128)(2,1)} %bitcast.17, f32[2560]{0:T(1024)} %refs_4_.1), custom_call_target="tpu_custom_call" | custom-call | flops 2621440 | bytes 2621440 | tf_op jit(solution)/shard_map/norm_key/pallas_call | solution.py:104
  3.6 0.0 copy-start.5
  3.6 4.4 %all-to-all-start.1 = ((bf16[4,2,5,2,64,128]{5,4,3,2,1,0:T(8,128)(2,1)}), bf16[4,2,5,2,64,128]{5,4,3,2,1,0:T(8,128)(2,1)S(1)}, u32[]{:S(2)}, u32[]{:S(2)}) async-start(bf16[4,2,5,2,64,128]{5,4,3,2,1,0:T(8,128)(2,1)} %norm_key.1), calls=%async_computation.1 | async-start | bytes 2621440 | tf_op jit(solution)/shard_map/all_to_all | solution.py:368
  8.1 0.1 pad_dynamic-slice_fusion
  8.2 0.1 copy.13
  8.2 0.7 reshape.22.a
  8.9 3.0 %plan.1.refs_0_ = s32[64]{0:T(128)} custom-call(s32[144]{0:T(256)} %reshape.22.a), custom_call_target="tpu_custom_call" | custom-call | flops 1000 | bytes 1000 | tf_op jit(solution)/shard_map/plan/pallas_call | solution.py:71
  12.0 1.9 %norm_query.1 = bf16[4,2,5,2,64,128]{5,4,3,2,1,0:T(8,128)(2,1)} custom-call(bf16[128,2560]{1,0:T(8,128)(2,1)S(1)} %bitcast.12, bf16[128,2560]{1,0:T(8,128)(2,1)S(1)} %bitcast.16, f32[2560]{0:T(1024)S(1)} %copy-done.5), custom_call_target="tpu_custom_call" | custom-call | flops 2621440 | bytes 2621440 | tf_op jit(solution)/shard_map/norm_query/pallas_call | solution.py:104
  13.9 12.1 %all-to-all-done.1.refs_1_.refs_2_ = bf16[4,2,5,2,64,128]{5,4,3,2,1,0:T(8,128)(2,1)S(1)} async-done(((bf16[4,2,5,2,64,128]{5,4,3,2,1,0:T(8,128)(2,1)}), bf16[4,2,5,2,64,128]{5,4,3,2,1,0:T(8,128)(2,1)S(1)}, u32[]{:S(2)}, u32[]{:S(2)}) %all-to-all-start.1) | async-done | bytes 1310752 | tf_op jit(solution)/shard_map/all_to_all | solution.py:368
  26.0 4.3 %all-to-all-start = ((bf16[4,2,5,2,64,128]{5,4,3,2,1,0:T(8,128)(2,1)}), bf16[4,2,5,2,64,128]{5,4,3,2,1,0:T(8,128)(2,1)}, u32[]{:S(2)}, u32[]{:S(2)}) async-start(bf16[4,2,5,2,64,128]{5,4,3,2,1,0:T(8,128)(2,1)} %norm_query.1), calls=%async_computation | async-start | bytes 2621440 | tf_op jit(solution)/shard_map/all_to_all | solution.py:368
  30.3 2.8 %pack.1 = (bf16[2,5,4,64,128]{4,3,2,1,0:T(8,128)(2,1)}, bf16[2,5,4,64,128]{4,3,2,1,0:T(8,128)(2,1)S(1)}) custom-call(s32[64]{0:T(128)S(1)} %copy-done.7, bf16[4,2,5,2,64,128]{5,4,3,2,1,0:T(8,128)(2,1)S(1)} %all-to-all-done.1.refs_1_.refs_2_), custom_call_target="tpu_custom_call" | custom-call | flops 1000 | bytes 2621440 | tf_op jit(solution)/shard_map/pack/pallas_call | solution.py:185
  33.1 1.9 %collective-permute-start = (bf16[2,5,4,64,128]{4,3,2,1,0:T(8,128)(2,1)}, bf16[2,5,4,64,128]{4,3,2,1,0:T(8,128)(2,1)S(1)}, u32[]{:S(2)}, u32[]{:S(2)}) collective-permute-start(bf16[2,5,4,64,128]{4,3,2,1,0:T(8,128)(2,1)} %get-tuple-element.24), channel_id=1, source_target_pairs={{0,32},{32,64},{64,96},{96,128},{128,160},{160,192},{192,224},{224... | collective-permute-start | bytes 1966088 | tf_op jit(solution)/shard_map/ppermute | solution.py:374
  35.0 3.6 %collective-permute-start.1 = (bf16[2,5,4,64,128]{4,3,2,1,0:T(8,128)(2,1)S(1)}, bf16[2,5,4,64,128]{4,3,2,1,0:T(8,128)(2,1)}, u32[]{:S(2)}, u32[]{:S(2)}) collective-permute-start(bf16[2,5,4,64,128]{4,3,2,1,0:T(8,128)(2,1)S(1)} %get-tuple-element.25), channel_id=1, source_target_pairs={{32,0},{64,32},{96,64},{128,96},{160,128},{192,160},{224,192},{256... | collective-permute-start | bytes 1966088 | tf_op jit(solution)/shard_map/ppermute | solution.py:374
  38.6 8.7 %all-to-all-done.refs_1_ = bf16[4,2,5,2,64,128]{5,4,3,2,1,0:T(8,128)(2,1)} async-done(((bf16[4,2,5,2,64,128]{5,4,3,2,1,0:T(8,128)(2,1)}), bf16[4,2,5,2,64,128]{5,4,3,2,1,0:T(8,128)(2,1)}, u32[]{:S(2)}, u32[]{:S(2)}) %all-to-all-start) | async-done | bytes 1310752 | tf_op jit(solution)/shard_map/all_to_all | solution.py:368
  47.4 0.0 collective-permute-done.refs_3_
  47.4 0.0 collective-permute-done.1.refs_4_
  47.4 0.8 copy-done.9
  48.2 12.1 %attend.1 = (bf16[4,5,2,64,128]{4,3,2,1,0:T(8,128)(2,1)S(1)}, bf16[4,2,5,2,64,128]{5,4,3,2,1,0:T(8,128)(2,1)}, bf16[2,5,4,64,128]{4,3,2,1,0:T(8,128)(2,1)}, bf16...) custom-call(s32[64]{0:T(128)S(1)} %copy-done.7, bf16[4,2,5,2,64,128]{5,4,3,2,1,0:T(8,128)(2,1)} %all-to-all-done.refs_1_, ...), custom_call_target="tpu_custom_call" | custom-call | flops 1509949440 | bytes 13107200 | tf_op jit(solution)/shard_map/attend/pallas_call | solution.py:337
  60.3 2.4 %collective-permute-start.2 = (bf16[2,5,4,64,128]{4,3,2,1,0:T(8,128)(2,1)}, bf16[2,5,4,64,128]{4,3,2,1,0:T(8,128)(2,1)S(1)}, u32[]{:S(2)}, u32[]{:S(2)}) collective-permute-start(bf16[2,5,4,64,128]{4,3,2,1,0:T(8,128)(2,1)} %get-tuple-element.28), channel_id=1, source_target_pairs={{32,0},{64,32},{96,64},{128,96},{160,128},{192,160},{224,192},{256... | collective-permute-start | bytes 1966088 | tf_op jit(solution)/shard_map/ppermute | solution.py:374
  62.7 4.3 %collective-permute-start.3 = (bf16[2,5,4,64,128]{4,3,2,1,0:T(8,128)(2,1)}, bf16[2,5,4,64,128]{4,3,2,1,0:T(8,128)(2,1)S(1)}, u32[]{:S(2)}, u32[]{:S(2)}) collective-permute-start(bf16[2,5,4,64,128]{4,3,2,1,0:T(8,128)(2,1)} %get-tuple-element.29), channel_id=1, source_target_pairs={{0,32},{32,64},{64,96},{96,128},{128,160},{160,192},{192,224},{224... | collective-permute-start | bytes 1966088 | tf_op jit(solution)/shard_map/ppermute | solution.py:374
  67.1 18.5 %all_to_all.20 = f32[8,16,128]{2,1,0:T(8,128)S(1)} all-to-all(f32[8,16,128]{2,1,0:T(8,128)S(1)} %broadcast_in_dim.15), channel_id=1, replica_groups=mesh['ctx'=16,'head'=4,'dp'=8] {'dp'}, dimensions={0} | all-to-all | bytes 131072 | tf_op jit(solution)/shard_map/all_to_all | solution.py:380
  85.6 0.0 collective-permute-done.2.refs_3_
  85.6 0.0 collective-permute-done.3.refs_4_
  85.6 1.3 %copy-done.3 = bf16[4,2,5,2,64,128]{5,4,3,2,1,0:T(8,128)(2,1)S(1)} copy-done((bf16[4,2,5,2,64,128]{5,4,3,2,1,0:T(8,128)(2,1)S(1)}, bf16[4,2,5,2,64,128]{5,4,3,2,1,0:T(8,128)(2,1)}, u32[]{:S(2)}) %copy-start.3) | copy-done | bytes 1310744
  86.9 1.6 %merge.1 = bf16[4,3,5,2,64,128]{5,4,3,2,1,0:T(8,128)(2,1)S(1)} custom-call(s32[64]{0:T(128)S(1)} %copy-done.7, bf16[4,5,2,64,128]{4,3,2,1,0:T(8,128)(2,1)S(1)} %get-tuple-element.26.refs_1_, bf16[4,2,5,2,64,128]{5,4,3,2,1,0:T(8,128)(2,1)S(1)} %copy-done.3, bf16[2,5,4,64,128]{4,3,2,1,0:T(8,128)(2,1)S(1)} %collective-permute-done.2.refs_3_, ...), custom_call_target="tpu_custom_call" | custom-call | flops 655360 | bytes 3932160 | tf_op jit(solution)/shard_map/merge/pallas_call | solution.py:214
  88.5 1.3 copy-done
  89.8 4.9 %all-to-all-start.3 = ((bf16[4,3,5,2,64,128]{5,4,3,2,1,0:T(8,128)(2,1)}), bf16[4,3,5,2,64,128]{5,4,3,2,1,0:T(8,128)(2,1)S(1)}, u32[]{:S(2)}, u32[]{:S(2)}) async-start(bf16[4,3,5,2,64,128]{5,4,3,2,1,0:T(8,128)(2,1)} %copy-done), calls=%async_computation.3 | async-start | bytes 3932160 | tf_op jit(solution)/shard_map/all_to_all | solution.py:368
  94.7 16.1 %all-gather = f32[256,128]{1,0:T(8,128)S(1)} all-gather(f32[16,128]{1,0:T(8,128)S(1)} %reduce_sum.18), channel_id=2, replica_groups=mesh['ctx'=16,'head'=4,'dp'=8] {'ctx'}, dimensions={0}, use_global_device_ids=true | all-gather | bytes 139264 | tf_op jit(solution)/shard_map/all_gather | solution.py:400
  110.8 15.0 %all-gather.1 = f32[64,128]{1,0:T(8,128)S(1)} all-gather(f32[16,128]{1,0:T(8,128)S(1)} %reduce_sum.19), channel_id=3, replica_groups=mesh['ctx'=16,'head'=4,'dp'=8] {'head'}, dimensions={0}, use_global_device_ids=true | all-gather | bytes 40960 | tf_op jit(solution)/shard_map/all_gather | solution.py:401
  125.9 0.6 divide_multiply_fusion
  126.5 0.0 all-to-all-done.3.refs_2_
  126.5 2.6 %unnorm.1 = (bf16[128,2560]{1,0:T(8,128)(2,1)}, bf16[128,2560]{1,0:T(8,128)(2,1)}, bf16[128,2560]{1,0:T(8,128)(2,1)}) custom-call(bf16[128,2560]{1,0:T(8,128)(2,1)S(1)} %bitcast.13, bf16[128,2560]{1,0:T(8,128)(2,1)S(1)} %bitcast.15, bf16[4,3,5,2,64,128]{5,4,3,2,1,0:T(8,128)(2,1)S(1)} %all-to-all-done.3.refs_2_, f32[2560]{0:T(1024)S(1)} %copy-done.5, ...), custom_call_target="tpu_custom_call" | custom-call | flops 7864320 | bytes 5242880 | tf_op jit(solution)/shard_map/unnorm/pallas_call | solution.py:155
  (24 shorter events, 0.1 us)
Async XLA Ops:
  3.6 4.5 %copy-start.8 = (s32[1,128,6]{1,0,2:T(1,128)S(1)}, s32[1,128,6]{1,0,2:T(1,128)}, u32[]{:S(2)}) copy-start(s32[1,128,6]{1,0,2:T(1,128)} %param.13) | copy-start | bytes 9220
  3.6 8.3 %copy-start.1 = (bf16[1,128,2560]{2,1,0:T(8,128)(2,1)S(1)}, bf16[1,128,2560]{2,1,0:T(8,128)(2,1)}, u32[]{:S(2)}) copy-start(bf16[1,128,2560]{2,1,0:T(8,128)(2,1)} %param.7) | copy-start | bytes 1966084
  3.6 8.3 %copy-start.4 = (bf16[1,128,2560]{2,1,0:T(8,128)(2,1)S(1)}, bf16[1,128,2560]{2,1,0:T(8,128)(2,1)}, u32[]{:S(2)}) copy-start(bf16[1,128,2560]{2,1,0:T(8,128)(2,1)} %param.10) | copy-start | bytes 1966084
  3.6 8.3 %copy-start.5 = (f32[2560]{0:T(1024)S(1)}, f32[2560]{0:T(1024)}, u32[]{:S(2)}) copy-start(f32[2560]{0:T(1024)} %refs_3_.1) | copy-start | bytes 30724
  3.6 22.3 %all-to-all-start.1 = ((bf16[4,2,5,2,64,128]{5,4,3,2,1,0:T(8,128)(2,1)}), bf16[4,2,5,2,64,128]{5,4,3,2,1,0:T(8,128)(2,1)S(1)}, u32[]{:S(2)}, u32[]{:S(2)}) async-start(bf16[4,2,5,2,64,128]{5,4,3,2,1,0:T(8,128)(2,1)} %norm_key.1), calls=%async_computation.1 | async-start | bytes 2621440 | tf_op jit(solution)/shard_map/all_to_all | solution.py:368
  13.9 16.4 %copy-start.7 = (s32[64]{0:T(128)S(1)}, s32[64]{0:T(128)}, u32[]{:S(2)}) copy-start(s32[64]{0:T(128)} %plan.1.refs_0_) | copy-start | bytes 772
  26.0 21.4 %all-to-all-start = ((bf16[4,2,5,2,64,128]{5,4,3,2,1,0:T(8,128)(2,1)}), bf16[4,2,5,2,64,128]{5,4,3,2,1,0:T(8,128)(2,1)}, u32[]{:S(2)}, u32[]{:S(2)}) async-start(bf16[4,2,5,2,64,128]{5,4,3,2,1,0:T(8,128)(2,1)} %norm_query.1), calls=%async_computation | async-start | bytes 2621440 | tf_op jit(solution)/shard_map/all_to_all | solution.py:368
  33.1 14.3 %collective-permute-start = (bf16[2,5,4,64,128]{4,3,2,1,0:T(8,128)(2,1)}, bf16[2,5,4,64,128]{4,3,2,1,0:T(8,128)(2,1)S(1)}, u32[]{:S(2)}, u32[]{:S(2)}) collective-permute-start(bf16[2,5,4,64,128]{4,3,2,1,0:T(8,128)(2,1)} %get-tuple-element.24), channel_id=1, source_target_pairs={{0,32},{32,64},{64,96},{96,128},{128,160},{160,192},{192,224},{224... | collective-permute-start | bytes 1966088 | tf_op jit(solution)/shard_map/ppermute | solution.py:374
  35.0 12.4 %collective-permute-start.1 = (bf16[2,5,4,64,128]{4,3,2,1,0:T(8,128)(2,1)S(1)}, bf16[2,5,4,64,128]{4,3,2,1,0:T(8,128)(2,1)}, u32[]{:S(2)}, u32[]{:S(2)}) collective-permute-start(bf16[2,5,4,64,128]{4,3,2,1,0:T(8,128)(2,1)S(1)} %get-tuple-element.25), channel_id=1, source_target_pairs={{32,0},{64,32},{96,64},{128,96},{160,128},{192,160},{224,192},{256... | collective-permute-start | bytes 1966088 | tf_op jit(solution)/shard_map/ppermute | solution.py:374
  47.4 0.8 copy-start.9
  60.3 25.2 %collective-permute-start.2 = (bf16[2,5,4,64,128]{4,3,2,1,0:T(8,128)(2,1)}, bf16[2,5,4,64,128]{4,3,2,1,0:T(8,128)(2,1)S(1)}, u32[]{:S(2)}, u32[]{:S(2)}) collective-permute-start(bf16[2,5,4,64,128]{4,3,2,1,0:T(8,128)(2,1)} %get-tuple-element.28), channel_id=1, source_target_pairs={{32,0},{64,32},{96,64},{128,96},{160,128},{192,160},{224,192},{256... | collective-permute-start | bytes 1966088 | tf_op jit(solution)/shard_map/ppermute | solution.py:374
  62.7 22.8 %collective-permute-start.3 = (bf16[2,5,4,64,128]{4,3,2,1,0:T(8,128)(2,1)}, bf16[2,5,4,64,128]{4,3,2,1,0:T(8,128)(2,1)S(1)}, u32[]{:S(2)}, u32[]{:S(2)}) collective-permute-start(bf16[2,5,4,64,128]{4,3,2,1,0:T(8,128)(2,1)} %get-tuple-element.29), channel_id=1, source_target_pairs={{0,32},{32,64},{64,96},{96,128},{128,160},{160,192},{192,224},{224... | collective-permute-start | bytes 1966088 | tf_op jit(solution)/shard_map/ppermute | solution.py:374
  85.6 1.3 %copy-start.3 = (bf16[4,2,5,2,64,128]{5,4,3,2,1,0:T(8,128)(2,1)S(1)}, bf16[4,2,5,2,64,128]{5,4,3,2,1,0:T(8,128)(2,1)}, u32[]{:S(2)}) copy-start(bf16[4,2,5,2,64,128]{5,4,3,2,1,0:T(8,128)(2,1)} %get-tuple-element.27.refs_2_) | copy-start | bytes 3932164
  88.5 1.3 copy-start
  89.8 36.0 %copy-start.6 = (f32[2560]{0:T(1024)S(1)}, f32[2560]{0:T(1024)}, u32[]{:S(2)}) copy-start(f32[2560]{0:T(1024)} %refs_4_.1) | copy-start | bytes 30724
  89.8 36.7 %copy-start.2 = (bf16[1,128,2560]{2,1,0:T(8,128)(2,1)S(1)}, bf16[1,128,2560]{2,1,0:T(8,128)(2,1)}, u32[]{:S(2)}) copy-start(bf16[1,128,2560]{2,1,0:T(8,128)(2,1)} %param.8) | copy-start | bytes 1966084
  89.8 36.7 %all-to-all-start.3 = ((bf16[4,3,5,2,64,128]{5,4,3,2,1,0:T(8,128)(2,1)}), bf16[4,3,5,2,64,128]{5,4,3,2,1,0:T(8,128)(2,1)S(1)}, u32[]{:S(2)}, u32[]{:S(2)}) async-start(bf16[4,3,5,2,64,128]{5,4,3,2,1,0:T(8,128)(2,1)} %copy-done), calls=%async_computation.3 | async-start | bytes 3932160 | tf_op jit(solution)/shard_map/all_to_all | solution.py:368

commit v2 on v1

--- a/solution.py
+++ b/solution.py
@@ -5,6 +5,7 @@
 from jax.experimental.pallas import tpu as pltpu
 from jax.sharding import PartitionSpec as P
 
+
 HD = 128
 TILE = 64
 ROWS = 16
@@ -42,6 +43,7 @@
     before, own, after = bits(0), bits(count), bits(2 * count)
     for i in range(16):
         plan_ref[count + i] = 0
+    plan_ref[count + 7] = listed_ref[3 * count]
     low, high, to_after, to_before = (jnp.int32(0),) * 4
     for b in range(blocks):
         slot_ref[b] = blocks + low
@@ -67,6 +69,7 @@
     start = lax.axis_index("ctx") * blocks
     padded = jnp.pad(key_tiles[0] - start, ((blocks, blocks), (0, 0)), constant_values=FAR)
     near = lax.dynamic_slice_in_dim(padded, start, 3 * blocks, 0).reshape(-1)
+    near = jnp.append(near, lax.axis_index("head"))
     count = blocks * listed
     return pl.pallas_call(
         lambda a, b, c: plan_kernel(a, b, c, blocks=blocks, listed=listed),
@@ -97,7 +100,7 @@
     lax.fori_loop(0, TILE // ROWS, step, 0)
 
 
-def norm_pack(x, y, gain, groups, name, grant):
+def norm_pack(x, y, gain, groups, grant):
     tokens, width = x.shape
     heads = width // HD // groups
     tiles = tokens // TILE
@@ -115,8 +118,50 @@
         ),
         compiler_params=room(grant),
         cost_estimate=cost(8 * tokens * width, 8 * tokens * width),
-        name=name,
     )(x, y, gain)
+
+
+def norm_turned_kernel(plan_ref, x_ref, y_ref, gain_ref, *outs, count, heads):
+    groups = len(outs)
+    width = groups * heads * HD
+    me = plan_ref[count + 7]
+
+    def step(c, carry):
+        rows = pl.ds(c * ROWS, ROWS)
+        x = x_ref[rows, :].astype(jnp.float32)
+        scaling = lax.rsqrt(jnp.sum(x * x, axis=-1, keepdims=True) / width + epsilon)
+        for s, out_ref in enumerate(outs):
+            start = lax.rem(me + s, groups) * (heads * HD)
+            for h in range(heads):
+                cols = pl.ds(pl.multiple_of(start + h * HD, HD), HD)
+                part = x_ref[rows, cols].astype(jnp.float32) * scaling * gain_ref[cols][None, :]
+                out_ref[0, h, 0, rows, :] = part.astype(jnp.bfloat16)
+                out_ref[1, h, 0, rows, :] = y_ref[rows, cols]
+        return carry
+
+    lax.fori_loop(0, TILE // ROWS, step, 0)
+
+
+def norm_turned(plan, x, y, gain, groups, count):
+    tokens, width = x.shape
+    heads = width // HD // groups
+    tiles = tokens // TILE
+    rows = pl.BlockSpec((TILE, width), lambda i: (i, 0))
+    return pl.pallas_call(
+        lambda *refs: norm_turned_kernel(*refs, count=count, heads=heads),
+        grid=(tiles,),
+        out_shape=[jax.ShapeDtypeStruct((2, heads, tiles, TILE, HD), jnp.bfloat16)] * groups,
+        in_specs=[
+            pl.BlockSpec(memory_space=pltpu.SMEM),
+            rows,
+            rows,
+            pl.BlockSpec((width,), lambda i: (0,)),
+        ],
+        out_specs=[pl.BlockSpec((2, heads, 1, TILE, HD), lambda i: (0, 0, i, 0, 0))] * groups,
+        compiler_params=room(16),
+        cost_estimate=cost(8 * tokens * width, 8 * tokens * width),
+        name="norm_query",
+    )(plan, x, y, gain)
 
 
 def unnorm_kernel(xq_ref, xk_ref, back_ref, gq_ref, gk_ref, oq_ref, ok_ref, ov_ref, *, groups, heads):
@@ -236,23 +281,17 @@
 
 def attend_kernel(
     plan_ref,
-    qd_ref,
     kv_ref,
     low_ref,
     high_ref,
-    dq_ref,
-    own_ref,
-    to_low_ref,
-    to_high_ref,
-    gain_ref,
-    keys_ref,
-    values_ref,
-    dk_ref,
-    dv_ref,
-    *,
+    *refs,
     blocks,
     listed,
 ):
+    qd_refs, refs = refs[: blocks // 2], refs[blocks // 2 :]
+    dq_ref, own_ref, to_low_ref, to_high_ref, gain_ref, keys_ref, values_ref, dk_ref, dv_ref = refs
+    groups = len(qd_refs)
+    me = plan_ref[blocks * listed + 7]
     scaling = HD**-0.5
     slots = blocks + 2 * SIDE
     for b in range(blocks):
@@ -273,10 +312,14 @@
 
     def together(first, gain_sum):
         tiles = range(GROUP)
-        at = [[plan_ref[(first + t) * listed + j] for j in range(listed)] for t in tiles]
-        where = [((first + t) // 2, (first + t) % 2) for t in tiles]
-        queries = [qd_ref[source, 0, 0, half] for source, half in where]
-        gradient = [qd_ref[source, 1, 0, half] for source, half in where]
+        far = [((first + t) // 2, (first + t) % 2) for t in tiles]
+        where = [(lax.rem(me - s + groups, groups), half) for s, half in far]
+        at = [
+            [plan_ref[(2 * source + half) * listed + j] for j in range(listed)]
+            for source, half in where
+        ]
+        queries = [qd_refs[s][0, 0, half] for s, half in far]
+        gradient = [qd_refs[s][1, 0, half] for s, half in far]
         keys = [jnp.concatenate([keys_ref[a] for a in at[t]], axis=0) for t in tiles]
         vals = [jnp.concatenate([values_ref[a] for a in at[t]], axis=0) for t in tiles]
         scores = [dot(keys[t], queries[t], ((1,), (1,))) for t in tiles]
@@ -344,7 +387,8 @@
             side,
             jax.ShapeDtypeStruct((16, HD), jnp.float32),
         ],
-        in_specs=[pl.BlockSpec(memory_space=pltpu.SMEM), block, block, side_spec, side_spec],
+        in_specs=[pl.BlockSpec(memory_space=pltpu.SMEM), block, side_spec, side_spec]
+        + [pl.BlockSpec((2, 1, tiles, TILE, HD), lambda h: (0, h, 0, 0, 0))] * groups,
         out_specs=[
             pl.BlockSpec((groups, 1, tiles, TILE, HD), lambda h: (0, h, 0, 0, 0)),
             block,
@@ -361,7 +405,7 @@
         compiler_params=room(24),
         cost_estimate=cost(12 * work * HD, 20 * kv.size, work),
         name="attend",
-    )(plan, qd, kv, low, high)
+    )(plan, kv, low, high, *qd)
 
 
 def swap(block):
@@ -372,6 +416,11 @@
     devices = range(lax.axis_size("ctx"))
     route = [(i - distance, i) for i in devices if i - distance in devices]
     return lax.ppermute(block, "ctx", route)
+
+
+def turn(block, distance):
+    count = lax.axis_size("head")
+    return lax.ppermute(block, "head", [(i, (i + distance) % count) for i in range(count)])
 
 
 def gathered(block, axis):
@@ -385,11 +434,14 @@
     blocks = groups * x_query.shape[1] // TILE
     listed = key_tiles.shape[2]
     count = blocks * listed
-    kv = swap(norm_pack(x_key[0], values[0], gain_key, groups, "norm_key", 60))
-    plan, gain = lax.optimization_barrier((make_plan(key_tiles, blocks), gain_query))
-    qd = swap(norm_pack(x_query[0], grad_out[0], gain, groups, "norm_query", 16))
+    kv = norm_pack(x_key[0], values[0], gain_key, groups, 60)
+    kv = swap(kv)
+    plan = make_plan(key_tiles, blocks)
+    qd = norm_turned(plan, x_query[0], grad_out[0], gain_query, groups, count)
+    qd = [qd[0]] + [turn(qd[s], s) for s in range(1, groups)]
     after, before = pack(plan, kv, count)
-    low, high = (in_hbm(side) for side in (shift(after, 1), shift(before, -1)))
+    low, high = shift(after, 1), shift(before, -1)
+    low, high = in_hbm(low), in_hbm(high)
     dq, own, to_low, to_high, gains = attend(plan, qd, kv, low, high, blocks, listed)
     from_after, from_before = shift(to_low, -1), shift(to_high, 1)
     gains = jnp.sum(gathered(gains, "dp"), axis=0)

time: 130 us -> 138 us (1.062)
  waiting for transfers between devices: 20.9 us -> 28.4 us
  Pallas kernels: 27 us -> 25.2 us
  starting transfers between devices: 25.8 us -> 27.3 us
    ppermute x0 -> x3, waiting for transfers between devices: none -> 14.4 us  [turn(): lax.ppermute(block, 'head', [(i, (i + distance) % count) for i in range(c...]
    ppermute x0 -> x3, starting transfers between devices: none -> 8.98 us  [turn(): lax.ppermute(block, 'head', [(i, (i + distance) % count) for i in range(c...]
    all_to_all x3 -> x2, waiting for transfers between devices: 20.8 us -> 13.9 us  [swap(): lax.all_to_all(block, 'head', split_axis=0, concat_axis=0, tiled=True)]
    all_to_all x3 -> x2, starting transfers between devices: 13.6 us -> 8.48 us  [swap(): lax.all_to_all(block, 'head', split_axis=0, concat_axis=0, tiled=True)]
    ppermute x4, starting transfers between devices: 12.3 us -> 9.88 us  [shift(): return lax.ppermute(block, 'ctx', route)]
    pallas_call x2 -> x1, Pallas kernels: 4.86 us -> 3.01 us  [norm_pack(): pl.pallas_call(lambda *refs: norm_kernel(*refs, groups=groups, heads=head...]
    pallas_call x0 -> x1, Pallas kernels: none -> 1.76 us  [norm_turned(): pl.pallas_call(lambda *refs: norm_turned_kernel(*refs, count=count, heads...]
    pallas_call x1, Pallas kernels: 2.78 us -> 1.13 us  [pack(): pl.pallas_call(lambda *refs: pack_kernel(*refs, count=count), grid=(heads...]
  transfers between devices with their start and end apart: 7 -> 9, of which waited for: 2 -> 3; matrix products, arithmetic and copies ran while one was open for 1% -> 1% of each run, Pallas kernels for 6% -> 3%
where the time goes in v2:
time: 138 us; the launch traced here: 137 us
  blocking collectives  49.7 us (36%)
  waiting for transfers between devices  28.4 us (21%)
  starting transfers between devices  27.3 us (20%)
  Pallas kernels  25.2 us (18%)
  local copies, waits for them, and re-layouts  4.6 us (3%)
    all_to_all x1, blocking collectives, gathered(): return lax.all_to_all(copies, axis, split_axis=0, concat_axis=0, tiled=True)  18.5 us
    all_gather x1, blocking collectives, per_device(): gains = jnp.sum(lax.all_gather(gains, 'ctx'), axis=0)  15.7 us
    all_gather x1, blocking collectives, per_device(): gains = lax.all_gather(gains, 'head')  15.6 us
    ppermute x3, waiting for transfers between devices, turn(): lax.ppermute(block, 'head', [(i, (i + distance) % count) for i in range(c...  14.4 us
    all_to_all x2, waiting for transfers between devices, swap(): lax.all_to_all(block, 'head', split_axis=0, concat_axis=0, tiled=True)  13.9 us
    pallas_call x1, Pallas kernels, attend(): pl.pallas_call(lambda *refs: attend_kernel(*refs, blocks=blocks, listed=l...  12 us
    ppermute x4, starting transfers between devices, shift(): return lax.ppermute(block, 'ctx', route)  9.88 us
    ppermute x3, starting transfers between devices, turn(): lax.ppermute(block, 'head', [(i, (i + distance) % count) for i in range(c...  8.98 us
  transfers between devices with their start and end apart: 9, of which 3 were waited for; matrix products, arithmetic and copies ran while one was open for 1% of the time, Pallas kernels for 3%

profile of v2, /device:TPU:24, one launch (start us, length us, event | category | flops | bytes accessed | tf_op | source)
XLA Modules:
  0.0 137.4 jit_solution(4432195948685215423)
XLA Ops:
  0.6 3.0 %shard_map.110 = bf16[4,2,5,2,64,128]{5,4,3,2,1,0:T(8,128)(2,1)} custom-call(bf16[128,2560]{1,0:T(8,128)(2,1)} %bitcast.13, bf16[128,2560]{1,0:T(8,128)(2,1)} %bitcast.18, f32[2560]{0:T(1024)} %refs_4_.1), custom_call_target="tpu_custom_call" | custom-call | flops 2621440 | bytes 2621440 | tf_op jit(solution)/shard_map/pallas_call | solution.py:107
  3.6 4.4 %all-to-all-start = ((bf16[4,2,5,2,64,128]{5,4,3,2,1,0:T(8,128)(2,1)}), bf16[4,2,5,2,64,128]{5,4,3,2,1,0:T(8,128)(2,1)S(1)}, u32[]{:S(2)}, u32[]{:S(2)}) async-start(bf16[4,2,5,2,64,128]{5,4,3,2,1,0:T(8,128)(2,1)} %shard_map.110), calls=%async_computation | async-start | bytes 2621440 | tf_op jit(solution)/shard_map/all_to_all | solution.py:412
  8.1 0.1 pad_dynamic-slice_fusion
  8.2 0.1 copy.13
  8.3 0.1 reshape.26
  8.4 0.6 pad_add_fusion.a
  9.0 3.0 %plan.1.refs_0_ = s32[64]{0:T(128)} custom-call(s32[145]{0:T(256)} %pad_add_fusion.a), custom_call_target="tpu_custom_call" | custom-call | flops 1000 | bytes 1000 | tf_op jit(solution)/shard_map/plan/pallas_call | solution.py:74
  12.1 13.9 %all-to-all-done.refs_1_ = bf16[4,2,5,2,64,128]{5,4,3,2,1,0:T(8,128)(2,1)S(1)} async-done(((bf16[4,2,5,2,64,128]{5,4,3,2,1,0:T(8,128)(2,1)}), bf16[4,2,5,2,64,128]{5,4,3,2,1,0:T(8,128)(2,1)S(1)}, u32[]{:S(2)}, u32[]{:S(2)}) %all-to-all-start) | async-done | bytes 1310752 | tf_op jit(solution)/shard_map/all_to_all | solution.py:412
  26.0 0.7 copy-done.7
  26.6 1.1 pack.1
  27.8 1.9 %collective-permute-start = (bf16[2,5,4,64,128]{4,3,2,1,0:T(8,128)(2,1)S(1)}, bf16[2,5,4,64,128]{4,3,2,1,0:T(8,128)(2,1)S(1)}, u32[]{:S(2)}, u32[]{:S(2)}) collective-permute-start(bf16[2,5,4,64,128]{4,3,2,1,0:T(8,128)(2,1)S(1)} %get-tuple-element.24), channel_id=1, source_target_pairs={{0,32},{32,64},{64,96},{96,128},{128,160},{160,192},{192,224},{224... | collective-permute-start | bytes 1966088 | tf_op jit(solution)/shard_map/ppermute | solution.py:418
  29.7 3.6 %collective-permute-start.1 = (bf16[2,5,4,64,128]{4,3,2,1,0:T(8,128)(2,1)S(1)}, bf16[2,5,4,64,128]{4,3,2,1,0:T(8,128)(2,1)S(1)}, u32[]{:S(2)}, u32[]{:S(2)}) collective-permute-start(bf16[2,5,4,64,128]{4,3,2,1,0:T(8,128)(2,1)S(1)} %get-tuple-element.25), channel_id=1, source_target_pairs={{32,0},{64,32},{96,64},{128,96},{160,128},{192,160},{224,192},{256... | collective-permute-start | bytes 1966088 | tf_op jit(solution)/shard_map/ppermute | solution.py:418
  33.4 1.8 %norm_query.1 = (bf16[2,5,2,64,128]{4,3,2,1,0:T(8,128)(2,1)S(1)}, bf16[2,5,2,64,128]{4,3,2,1,0:T(8,128)(2,1)S(1)}, bf16[2,5,2,64,128]{4,3,2,1,0:T(8,128)(2,1)S(1)}, bf16[2,5,2,64,128]{4,3,2,1,0:T(8,128)(2,1)S(1)}) custom-call(s32[64]{0:T(128)S(1)} %copy-done.7, bf16[128,2560]{1,0:T(8,128)(2,1)S(1)} %bitcast.15, bf16[128,2560]{1,0:T(8,128)(2,1)S(1)} %bitcast.17, ...), custom_call_target="tpu_custom_call" | custom-call | flops 2621440 | bytes 2621440 | tf_op jit(solution)/shard_map/norm_query/pallas_call | solution.py:150
  35.1 2.5 %collective-permute-start.2 = (bf16[2,5,2,64,128]{4,3,2,1,0:T(8,128)(2,1)S(1)}, bf16[2,5,2,64,128]{4,3,2,1,0:T(8,128)(2,1)S(1)}, u32[]{:S(2)}, u32[]{:S(2)}) collective-permute-start(bf16[2,5,2,64,128]{4,3,2,1,0:T(8,128)(2,1)S(1)} %get-tuple-element.27), channel_id=1, source_target_pairs={{0,8},{8,16},{16,24},{24,0},{1,9},{9,17},{17,25},{25,1},{2,10},{10... | collective-permute-start | bytes 983048 | tf_op jit(solution)/shard_map/ppermute | solution.py:423
  37.6 4.0 %collective-permute-start.3 = (bf16[2,5,2,64,128]{4,3,2,1,0:T(8,128)(2,1)S(1)}, bf16[2,5,2,64,128]{4,3,2,1,0:T(8,128)(2,1)S(1)}, u32[]{:S(2)}, u32[]{:S(2)}) collective-permute-start(bf16[2,5,2,64,128]{4,3,2,1,0:T(8,128)(2,1)S(1)} %get-tuple-element.28), channel_id=1, source_target_pairs={{0,16},{8,24},{16,0},{24,8},{1,17},{9,25},{17,1},{25,9},{2,18},{10... | collective-permute-start | bytes 983048 | tf_op jit(solution)/shard_map/ppermute | solution.py:423
  41.6 2.5 %collective-permute-start.4 = (bf16[2,5,2,64,128]{4,3,2,1,0:T(8,128)(2,1)S(1)}, bf16[2,5,2,64,128]{4,3,2,1,0:T(8,128)(2,1)S(1)}, u32[]{:S(2)}, u32[]{:S(2)}) collective-permute-start(bf16[2,5,2,64,128]{4,3,2,1,0:T(8,128)(2,1)S(1)} %get-tuple-element.29), channel_id=1, source_target_pairs={{0,24},{8,0},{16,8},{24,16},{1,25},{9,1},{17,9},{25,17},{2,26},{10... | collective-permute-start | bytes 983048 | tf_op jit(solution)/shard_map/ppermute | solution.py:423
  44.1 11.5 %collective-permute-done.2.refs_5_ = bf16[2,5,2,64,128]{4,3,2,1,0:T(8,128)(2,1)S(1)} collective-permute-done((bf16[2,5,2,64,128]{4,3,2,1,0:T(8,128)(2,1)S(1)}, bf16[2,5,2,64,128]{4,3,2,1,0:T(8,128)(2,1)S(1)}, u32[]{:S(2)}, u32[]{:S(2)}) %collective-permute-start.2) | collective-permute-done | bytes 327712 | tf_op jit(solution)/shard_map/ppermute | solution.py:423
  55.7 2.9 %collective-permute-done.4.refs_7_ = bf16[2,5,2,64,128]{4,3,2,1,0:T(8,128)(2,1)S(1)} collective-permute-done((bf16[2,5,2,64,128]{4,3,2,1,0:T(8,128)(2,1)S(1)}, bf16[2,5,2,64,128]{4,3,2,1,0:T(8,128)(2,1)S(1)}, u32[]{:S(2)}, u32[]{:S(2)}) %collective-permute-start.4) | collective-permute-done | bytes 327712 | tf_op jit(solution)/shard_map/ppermute | solution.py:423
  58.6 0.8 copy-done.9
  59.4 0.2 copy-done.10
  59.6 12.0 %attend.1 = (bf16[4,5,2,64,128]{4,3,2,1,0:T(8,128)(2,1)S(1)}, bf16[4,2,5,2,64,128]{5,4,3,2,1,0:T(8,128)(2,1)}, bf16[2,5,4,64,128]{4,3,2,1,0:T(8,128)(2,1)}, bf16...) custom-call(s32[64]{0:T(128)S(1)} %copy-done.7, bf16[4,2,5,2,64,128]{5,4,3,2,1,0:T(8,128)(2,1)S(1)} %all-to-all-done.refs_1_, ...), custom_call_target="tpu_custom_call" | custom-call | flops 1509949440 | bytes 13107200 | tf_op jit(solution)/shard_map/attend/pallas_call | solution.py:380
  71.7 1.9 %collective-permute-start.5 = (bf16[2,5,4,64,128]{4,3,2,1,0:T(8,128)(2,1)}, bf16[2,5,4,64,128]{4,3,2,1,0:T(8,128)(2,1)S(1)}, u32[]{:S(2)}, u32[]{:S(2)}) collective-permute-start(bf16[2,5,4,64,128]{4,3,2,1,0:T(8,128)(2,1)} %get-tuple-element.32), channel_id=1, source_target_pairs={{32,0},{64,32},{96,64},{128,96},{160,128},{192,160},{224,192},{256... | collective-permute-start | bytes 1966088 | tf_op jit(solution)/shard_map/ppermute | solution.py:418
  73.6 2.4 %collective-permute-start.6 = (bf16[2,5,4,64,128]{4,3,2,1,0:T(8,128)(2,1)}, bf16[2,5,4,64,128]{4,3,2,1,0:T(8,128)(2,1)S(1)}, u32[]{:S(2)}, u32[]{:S(2)}) collective-permute-start(bf16[2,5,4,64,128]{4,3,2,1,0:T(8,128)(2,1)} %get-tuple-element.33), channel_id=1, source_target_pairs={{0,32},{32,64},{64,96},{96,128},{128,160},{160,192},{192,224},{224... | collective-permute-start | bytes 1966088 | tf_op jit(solution)/shard_map/ppermute | solution.py:418
  76.0 18.5 %all_to_all.15 = f32[8,16,128]{2,1,0:T(8,128)S(1)} all-to-all(f32[8,16,128]{2,1,0:T(8,128)S(1)} %broadcast_in_dim.15), channel_id=1, replica_groups=mesh['ctx'=16,'head'=4,'dp'=8] {'dp'}, dimensions={0} | all-to-all | bytes 131072 | tf_op jit(solution)/shard_map/all_to_all | solution.py:429
  94.5 1.3 copy-done.3
  95.8 1.6 %merge.1 = bf16[4,3,5,2,64,128]{5,4,3,2,1,0:T(8,128)(2,1)S(1)} custom-call(s32[64]{0:T(128)S(1)} %copy-done.7, bf16[4,5,2,64,128]{4,3,2,1,0:T(8,128)(2,1)S(1)} %get-tuple-element.30.refs_1_, bf16[4,2,5,2,64,128]{5,4,3,2,1,0:T(8,128)(2,1)S(1)} %copy-done.3, bf16[2,5,4,64,128]{4,3,2,1,0:T(8,128)(2,1)S(1)} %collective-permute-done.5.refs_3_, ...), custom_call_target="tpu_custom_call" | custom-call | flops 655360 | bytes 3932160 | tf_op jit(solution)/shard_map/merge/pallas_call | solution.py:259
  97.5 1.3 copy-done
  98.8 4.1 %all-to-all-start.2 = ((bf16[4,3,5,2,64,128]{5,4,3,2,1,0:T(8,128)(2,1)}), bf16[4,3,5,2,64,128]{5,4,3,2,1,0:T(8,128)(2,1)S(1)}, u32[]{:S(2)}, u32[]{:S(2)}) async-start(bf16[4,3,5,2,64,128]{5,4,3,2,1,0:T(8,128)(2,1)} %copy-done), calls=%async_computation.2 | async-start | bytes 3932160 | tf_op jit(solution)/shard_map/all_to_all | solution.py:412
  102.8 15.7 %all-gather = f32[256,128]{1,0:T(8,128)S(1)} all-gather(f32[16,128]{1,0:T(8,128)S(1)} %reduce_sum.18), channel_id=2, replica_groups=mesh['ctx'=16,'head'=4,'dp'=8] {'ctx'}, dimensions={0}, use_global_device_ids=true | all-gather | bytes 139264 | tf_op jit(solution)/shard_map/all_gather | solution.py:452
  118.5 15.6 %all-gather.1 = f32[64,128]{1,0:T(8,128)S(1)} all-gather(f32[16,128]{1,0:T(8,128)S(1)} %reduce_sum.19), channel_id=3, replica_groups=mesh['ctx'=16,'head'=4,'dp'=8] {'head'}, dimensions={0}, use_global_device_ids=true | all-gather | bytes 40960 | tf_op jit(solution)/shard_map/all_gather | solution.py:453
  134.1 0.6 divide_multiply_fusion
  134.8 2.6 %unnorm.1 = (bf16[128,2560]{1,0:T(8,128)(2,1)}, bf16[128,2560]{1,0:T(8,128)(2,1)}, bf16[128,2560]{1,0:T(8,128)(2,1)}) custom-call(bf16[128,2560]{1,0:T(8,128)(2,1)S(1)} %bitcast.16, bf16[128,2560]{1,0:T(8,128)(2,1)S(1)} %bitcast.14, bf16[4,3,5,2,64,128]{5,4,3,2,1,0:T(8,128)(2,1)S(1)} %all-to-all-done.2.refs_2_, f32[2560]{0:T(1024)S(1)} %copy-done.6, ...), custom_call_target="tpu_custom_call" | custom-call | flops 7864320 | bytes 5242880 | tf_op jit(solution)/shard_map/unnorm/pallas_call | solution.py:200
  (31 shorter events, 0.1 us)
Async XLA Ops:
  3.6 4.4 %copy-start.8 = (s32[1,128,6]{1,0,2:T(1,128)S(1)}, s32[1,128,6]{1,0,2:T(1,128)}, u32[]{:S(2)}) copy-start(s32[1,128,6]{1,0,2:T(1,128)} %param.13) | copy-start | bytes 9220
  3.6 22.3 %all-to-all-start = ((bf16[4,2,5,2,64,128]{5,4,3,2,1,0:T(8,128)(2,1)}), bf16[4,2,5,2,64,128]{5,4,3,2,1,0:T(8,128)(2,1)S(1)}, u32[]{:S(2)}, u32[]{:S(2)}) async-start(bf16[4,2,5,2,64,128]{5,4,3,2,1,0:T(8,128)(2,1)} %shard_map.110), calls=%async_computation | async-start | bytes 2621440 | tf_op jit(solution)/shard_map/all_to_all | solution.py:412
  8.1 25.3 %copy-start.2 = (bf16[1,128,2560]{2,1,0:T(8,128)(2,1)S(1)}, bf16[1,128,2560]{2,1,0:T(8,128)(2,1)}, u32[]{:S(2)}) copy-start(bf16[1,128,2560]{2,1,0:T(8,128)(2,1)} %param.7) | copy-start | bytes 1966084
  8.1 25.3 %copy-start.4 = (bf16[1,128,2560]{2,1,0:T(8,128)(2,1)S(1)}, bf16[1,128,2560]{2,1,0:T(8,128)(2,1)}, u32[]{:S(2)}) copy-start(bf16[1,128,2560]{2,1,0:T(8,128)(2,1)} %param.10) | copy-start | bytes 1966084
  8.1 25.3 %copy-start.6 = (f32[2560]{0:T(1024)S(1)}, f32[2560]{0:T(1024)}, u32[]{:S(2)}) copy-start(f32[2560]{0:T(1024)} %refs_3_.3) | copy-start | bytes 30724
  26.0 0.7 copy-start.7
  27.8 30.8 %collective-permute-start = (bf16[2,5,4,64,128]{4,3,2,1,0:T(8,128)(2,1)S(1)}, bf16[2,5,4,64,128]{4,3,2,1,0:T(8,128)(2,1)S(1)}, u32[]{:S(2)}, u32[]{:S(2)}) collective-permute-start(bf16[2,5,4,64,128]{4,3,2,1,0:T(8,128)(2,1)S(1)} %get-tuple-element.24), channel_id=1, source_target_pairs={{0,32},{32,64},{64,96},{96,128},{128,160},{160,192},{192,224},{224... | collective-permute-start | bytes 1966088 | tf_op jit(solution)/shard_map/ppermute | solution.py:418
  29.7 28.9 %collective-permute-start.1 = (bf16[2,5,4,64,128]{4,3,2,1,0:T(8,128)(2,1)S(1)}, bf16[2,5,4,64,128]{4,3,2,1,0:T(8,128)(2,1)S(1)}, u32[]{:S(2)}, u32[]{:S(2)}) collective-permute-start(bf16[2,5,4,64,128]{4,3,2,1,0:T(8,128)(2,1)S(1)} %get-tuple-element.25), channel_id=1, source_target_pairs={{32,0},{64,32},{96,64},{128,96},{160,128},{192,160},{224,192},{256... | collective-permute-start | bytes 1966088 | tf_op jit(solution)/shard_map/ppermute | solution.py:418
  35.1 20.5 %collective-permute-start.2 = (bf16[2,5,2,64,128]{4,3,2,1,0:T(8,128)(2,1)S(1)}, bf16[2,5,2,64,128]{4,3,2,1,0:T(8,128)(2,1)S(1)}, u32[]{:S(2)}, u32[]{:S(2)}) collective-permute-start(bf16[2,5,2,64,128]{4,3,2,1,0:T(8,128)(2,1)S(1)} %get-tuple-element.27), channel_id=1, source_target_pairs={{0,8},{8,16},{16,24},{24,0},{1,9},{9,17},{17,25},{25,1},{2,10},{10... | collective-permute-start | bytes 983048 | tf_op jit(solution)/shard_map/ppermute | solution.py:423
  37.6 18.0 %collective-permute-start.3 = (bf16[2,5,2,64,128]{4,3,2,1,0:T(8,128)(2,1)S(1)}, bf16[2,5,2,64,128]{4,3,2,1,0:T(8,128)(2,1)S(1)}, u32[]{:S(2)}, u32[]{:S(2)}) collective-permute-start(bf16[2,5,2,64,128]{4,3,2,1,0:T(8,128)(2,1)S(1)} %get-tuple-element.28), channel_id=1, source_target_pairs={{0,16},{8,24},{16,0},{24,8},{1,17},{9,25},{17,1},{25,9},{2,18},{10... | collective-permute-start | bytes 983048 | tf_op jit(solution)/shard_map/ppermute | solution.py:423
  41.6 17.0 %collective-permute-start.4 = (bf16[2,5,2,64,128]{4,3,2,1,0:T(8,128)(2,1)S(1)}, bf16[2,5,2,64,128]{4,3,2,1,0:T(8,128)(2,1)S(1)}, u32[]{:S(2)}, u32[]{:S(2)}) collective-permute-start(bf16[2,5,2,64,128]{4,3,2,1,0:T(8,128)(2,1)S(1)} %get-tuple-element.29), channel_id=1, source_target_pairs={{0,24},{8,0},{16,8},{24,16},{1,25},{9,1},{17,9},{25,17},{2,26},{10... | collective-permute-start | bytes 983048 | tf_op jit(solution)/shard_map/ppermute | solution.py:423
  58.6 0.8 copy-start.9
  58.6 1.0 copy-start.10
  71.7 22.9 %collective-permute-start.5 = (bf16[2,5,4,64,128]{4,3,2,1,0:T(8,128)(2,1)}, bf16[2,5,4,64,128]{4,3,2,1,0:T(8,128)(2,1)S(1)}, u32[]{:S(2)}, u32[]{:S(2)}) collective-permute-start(bf16[2,5,4,64,128]{4,3,2,1,0:T(8,128)(2,1)} %get-tuple-element.32), channel_id=1, source_target_pairs={{32,0},{64,32},{96,64},{128,96},{160,128},{192,160},{224,192},{256... | collective-permute-start | bytes 1966088 | tf_op jit(solution)/shard_map/ppermute | solution.py:418
  73.6 20.9 %collective-permute-start.6 = (bf16[2,5,4,64,128]{4,3,2,1,0:T(8,128)(2,1)}, bf16[2,5,4,64,128]{4,3,2,1,0:T(8,128)(2,1)S(1)}, u32[]{:S(2)}, u32[]{:S(2)}) collective-permute-start(bf16[2,5,4,64,128]{4,3,2,1,0:T(8,128)(2,1)} %get-tuple-element.33), channel_id=1, source_target_pairs={{0,32},{32,64},{64,96},{96,128},{128,160},{160,192},{192,224},{224... | collective-permute-start | bytes 1966088 | tf_op jit(solution)/shard_map/ppermute | solution.py:418
  94.5 1.3 copy-start.3
  97.5 1.3 copy-start
  98.8 35.3 %copy-start.5 = (f32[2560]{0:T(1024)S(1)}, f32[2560]{0:T(1024)}, u32[]{:S(2)}) copy-start(f32[2560]{0:T(1024)} %refs_4_.1) | copy-start | bytes 30724
  98.8 36.0 %copy-start.1 = (bf16[1,128,2560]{2,1,0:T(8,128)(2,1)S(1)}, bf16[1,128,2560]{2,1,0:T(8,128)(2,1)}, u32[]{:S(2)}) copy-start(bf16[1,128,2560]{2,1,0:T(8,128)(2,1)} %param.8) | copy-start | bytes 1966084
  98.8 36.0 %all-to-all-start.2 = ((bf16[4,3,5,2,64,128]{5,4,3,2,1,0:T(8,128)(2,1)}), bf16[4,3,5,2,64,128]{5,4,3,2,1,0:T(8,128)(2,1)S(1)}, u32[]{:S(2)}, u32[]{:S(2)}) async-start(bf16[4,3,5,2,64,128]{5,4,3,2,1,0:T(8,128)(2,1)} %copy-done), calls=%async_computation.2 | async-start | bytes 3932160 | tf_op jit(solution)/shard_map/all_to_all | solution.py:412

commit v3 on v2

--- a/solution.py
+++ b/solution.py
@@ -164,7 +164,23 @@
     )(plan, x, y, gain)
 
 
-def unnorm_kernel(xq_ref, xk_ref, back_ref, gq_ref, gk_ref, oq_ref, ok_ref, ov_ref, *, groups, heads):
+def unnorm_kernel(
+    xq_ref,
+    xk_ref,
+    back_ref,
+    gq_ref,
+    gk_ref,
+    sums_ref,
+    oq_ref,
+    ok_ref,
+    ov_ref,
+    sq_ref,
+    sk_ref,
+    *,
+    groups,
+    heads,
+    samples,
+):
     width = groups * heads * HD
     places = [(g, h, slice((g * heads + h) * HD, (g * heads + h + 1) * HD)) for g in range(groups) for h in range(heads)]
 
@@ -191,28 +207,36 @@
 
     lax.fori_loop(0, TILE // ROWS, step, 0)
 
-
-def unnorm(xq, xk, back, gain_query, gain_key):
+    @pl.when(pl.program_id(0) == 0)
+    def _():
+        for row, gain_ref, out_ref in ((0, gq_ref, sq_ref), (8, gk_ref, sk_ref)):
+            for g, h, cols in places:
+                out_ref[cols] = sums_ref[g, row + h] / gain_ref[cols] / samples
+
+
+def unnorm(xq, xk, back, gain_query, gain_key, sums, samples):
     tokens, width = xq.shape
     groups, _, heads = back.shape[:3]
     rows = pl.BlockSpec((TILE, width), lambda i: (i, 0))
     gain = pl.BlockSpec((width,), lambda i: (0,))
-    return pl.pallas_call(
-        lambda *refs: unnorm_kernel(*refs, groups=groups, heads=heads),
+    total = jax.ShapeDtypeStruct((width,), jnp.float32)
+    return pl.pallas_call(
+        lambda *refs: unnorm_kernel(*refs, groups=groups, heads=heads, samples=samples),
         grid=(tokens // TILE,),
-        out_shape=[jax.ShapeDtypeStruct((tokens, width), jnp.bfloat16)] * 3,
+        out_shape=[jax.ShapeDtypeStruct((tokens, width), jnp.bfloat16)] * 3 + [total] * 2,
         in_specs=[
             rows,
             rows,
             pl.BlockSpec((groups, 3, heads, 1, TILE, HD), lambda i: (0, 0, 0, i, 0, 0)),
             gain,
             gain,
-        ],
-        out_specs=[rows] * 3,
+            pl.BlockSpec(sums.shape, lambda i: (0, 0, 0)),
+        ],
+        out_specs=[rows] * 3 + [gain] * 2,
         compiler_params=room(16),
         cost_estimate=cost(24 * tokens * width, 16 * tokens * width),
         name="unnorm",
-    )(xq, xk, back, gain_query, gain_key)
+    )(xq, xk, back, gain_query, gain_key, sums)
 
 
 def pack_kernel(plan_ref, kv_ref, after_ref, before_ref, *, count):
@@ -242,7 +266,23 @@
     )(plan, kv)
 
 
-def merge_kernel(plan_ref, dq_ref, own_ref, after_ref, before_ref, out_ref, total_ref, *, count):
+def merge_kernel(
+    plan_ref,
+    dq_ref,
+    own_ref,
+    after_ref,
+    before_ref,
+    parts_ref,
+    out_ref,
+    sum_ref,
+    total_ref,
+    *,
+    count,
+):
+    @pl.when(pl.program_id(0) == 0)
+    def _():
+        sum_ref[...] = jnp.sum(parts_ref[...], axis=0)
+
     total_ref[...] = own_ref[:, :, 0].astype(jnp.float32)
     for which, side_ref in ((0, after_ref), (8, before_ref)):
         for r in range(SIDE):
@@ -253,26 +293,33 @@
     out_ref[:, 1:, 0] = total_ref[...].astype(jnp.bfloat16)
 
 
-def merge(plan, dq, own, after, before, count):
+def merge(plan, dq, own, after, before, parts, count):
     groups, _, heads, tiles, _, _ = own.shape
     side_spec = pl.BlockSpec((2, 1, SIDE, TILE, HD), lambda h: (0, h, 0, 0, 0))
     return pl.pallas_call(
         lambda *refs: merge_kernel(*refs, count=count),
         grid=(heads,),
-        out_shape=jax.ShapeDtypeStruct((groups, 3, heads, tiles, TILE, HD), jnp.bfloat16),
+        out_shape=[
+            pltpu.HBM((groups, 3, heads, tiles, TILE, HD), jnp.bfloat16),
+            jax.ShapeDtypeStruct(parts.shape[1:], jnp.float32),
+        ],
         in_specs=[
             pl.BlockSpec(memory_space=pltpu.SMEM),
             pl.BlockSpec((groups, 1, tiles, TILE, HD), lambda h: (0, h, 0, 0, 0)),
             pl.BlockSpec((groups, 2, 1, tiles, TILE, HD), lambda h: (0, 0, h, 0, 0, 0)),
             side_spec,
             side_spec,
-        ],
-        out_specs=pl.BlockSpec((groups, 3, 1, tiles, TILE, HD), lambda h: (0, 0, h, 0, 0, 0)),
+            pl.BlockSpec(parts.shape, lambda h: (0, 0, 0)),
+        ],
+        out_specs=[
+            pl.BlockSpec((groups, 3, 1, tiles, TILE, HD), lambda h: (0, 0, h, 0, 0, 0)),
+            pl.BlockSpec(parts.shape[1:], lambda h: (0, 0)),
+        ],
         scratch_shapes=[pltpu.VMEM((groups, 2, tiles, TILE, HD), jnp.float32)],
         compiler_params=room(8),
         cost_estimate=cost(own.size, 6 * own.size),
         name="merge",
-    )(plan, dq, own, after, before)
+    )(plan, dq, own, after, before, parts)
 
 
 def dot(a, b, dims):
@@ -367,10 +414,12 @@
             out_ref[1, 0, r] = dv_ref[s].astype(jnp.bfloat16)
     head = pl.program_id(0)
     for which, part in ((0, gain_query), (8, gain_key)):
-        gain_ref[pl.ds(which + head, 1)] = jnp.sum(part, axis=0, keepdims=True)
-
-
-def attend(plan, qd, kv, low, high, blocks, listed):
+        row = jnp.sum(part, axis=0, keepdims=True)
+        for copy in range(gain_ref.shape[0]):
+            gain_ref[copy, pl.ds(which + head, 1)] = row
+
+
+def attend(plan, qd, kv, low, high, blocks, listed, copies):
     groups, _, heads, tiles, _, _ = kv.shape
     slots = blocks + 2 * SIDE
     side = jax.ShapeDtypeStruct(low.shape, jnp.bfloat16)
@@ -385,7 +434,7 @@
             pltpu.HBM(kv.shape, jnp.bfloat16),
             side,
             side,
-            jax.ShapeDtypeStruct((16, HD), jnp.float32),
+            jax.ShapeDtypeStruct((copies, 16, HD), jnp.float32),
         ],
         in_specs=[pl.BlockSpec(memory_space=pltpu.SMEM), block, side_spec, side_spec]
         + [pl.BlockSpec((2, 1, tiles, TILE, HD), lambda h: (0, h, 0, 0, 0))] * groups,
@@ -394,7 +443,7 @@
             block,
             side_spec,
             side_spec,
-            pl.BlockSpec((16, HD), lambda h: (0, 0)),
+            pl.BlockSpec((copies, 16, HD), lambda h: (0, 0, 0)),
         ],
         scratch_shapes=[
             pltpu.VMEM((slots, TILE, HD), jnp.bfloat16),
@@ -421,12 +470,6 @@
 def turn(block, distance):
     count = lax.axis_size("head")
     return lax.ppermute(block, "head", [(i, (i + distance) % count) for i in range(count)])
-
-
-def gathered(block, axis):
-    count = lax.axis_size(axis)
-    copies = jnp.broadcast_to(block[None], (count,) + block.shape)
-    return lax.all_to_all(copies, axis, split_axis=0, concat_axis=0, tiled=True)
 
 
 def per_device(x_query, x_key, values, grad_out, gain_query, gain_key, key_tiles):
@@ -442,28 +485,20 @@
     after, before = pack(plan, kv, count)
     low, high = shift(after, 1), shift(before, -1)
     low, high = in_hbm(low), in_hbm(high)
-    dq, own, to_low, to_high, gains = attend(plan, qd, kv, low, high, blocks, listed)
+    dq, own, to_low, to_high, gains = attend(
+        plan, qd, kv, low, high, blocks, listed, lax.axis_size("dp")
+    )
     from_after, from_before = shift(to_low, -1), shift(to_high, 1)
-    gains = jnp.sum(gathered(gains, "dp"), axis=0)
+    gains = lax.all_to_all(gains, "dp", split_axis=0, concat_axis=0, tiled=True)
     from_after, from_before, gains = lax.optimization_barrier((from_after, from_before, gains))
-    merged = merge(plan, dq, own, from_after, from_before, count)
-    merged, gains = lax.optimization_barrier((merged, gains))
+    merged, gains = merge(plan, dq, in_hbm(own), from_after, from_before, gains, count)
     back = swap(merged)
     gains = jnp.sum(lax.all_gather(gains, "ctx"), axis=0)
     gains = lax.all_gather(gains, "head")
-    grad_x_query, grad_x_key, grad_values = unnorm(
-        x_query[0], x_key[0], back, gain_query, gain_key
+    grad_x_query, grad_x_key, grad_values, sum_query, sum_key = unnorm(
+        x_query[0], x_key[0], back, gain_query, gain_key, gains, lax.axis_size("dp")
     )
-    heads = x_query.shape[2] // HD // groups
-    gains = [gains[:, at : at + heads].reshape(-1) for at in (0, 8)]
-    samples = lax.axis_size("dp")
-    return (
-        grad_x_query[None],
-        grad_x_key[None],
-        grad_values[None],
-        gains[0] / gain_query / samples,
-        gains[1] / gain_key / samples,
-    )
+    return grad_x_query[None], grad_x_key[None], grad_values[None], sum_query, sum_key
 
 
 def solution(mesh):

time: 138 us -> 138 us (level)
  Pallas kernels: 25.2 us -> 28.2 us
  local copies, waits for them, and re-layouts: 4.6 us -> 1.99 us
    pallas_call x1, Pallas kernels: 1.63 us -> 4.46 us  [merge(): pl.pallas_call(lambda *refs: merge_kernel(*refs, count=count), grid=(head...]
    unnamed x23 -> x21, local copies, waits for them, and re-layouts: 4.32 us -> 1.72 us
where the time goes in v3:
time: 138 us; the launch traced here: 137 us
  blocking collectives  49.7 us (36%)
  waiting for transfers between devices  28.4 us (21%)
  Pallas kernels  28.2 us (20%)
  starting transfers between devices  27.3 us (20%)
  local copies, waits for them, and re-layouts  1.99 us (1%)
    all_to_all x1, blocking collectives, per_device(): gains = lax.all_to_all(gains, 'dp', split_axis=0, concat_axis=0, tiled=True)  18.5 us
    all_gather x1, blocking collectives, per_device(): gains = jnp.sum(lax.all_gather(gains, 'ctx'), axis=0)  15.7 us
    all_gather x1, blocking collectives, per_device(): gains = lax.all_gather(gains, 'head')  15.6 us
    ppermute x3, waiting for transfers between devices, turn(): lax.ppermute(block, 'head', [(i, (i + distance) % count) for i in range(c...  14.4 us
    all_to_all x2, waiting for transfers between devices, swap(): lax.all_to_all(block, 'head', split_axis=0, concat_axis=0, tiled=True)  13.9 us
    pallas_call x1, Pallas kernels, attend(): pl.pallas_call(lambda *refs: attend_kernel(*refs, blocks=blocks, listed=l...  12.2 us
    ppermute x4, starting transfers between devices, shift(): return lax.ppermute(block, 'ctx', route)  9.88 us
    ppermute x3, starting transfers between devices, turn(): lax.ppermute(block, 'head', [(i, (i + distance) % count) for i in range(c...  8.97 us
  transfers between devices with their start and end apart: 9, of which 3 were waited for; matrix products, arithmetic and copies ran while one was open for 1% of the time, Pallas kernels for 3%

profile of v3, /device:TPU:24, one launch (start us, length us, event | category | flops | bytes accessed | tf_op | source)
XLA Modules:
  0.0 137.1 jit_solution(12406152832070413394)
XLA Ops:
  0.6 3.0 %shard_map.110 = bf16[4,2,5,2,64,128]{5,4,3,2,1,0:T(8,128)(2,1)} custom-call(bf16[128,2560]{1,0:T(8,128)(2,1)} %bitcast.13, bf16[128,2560]{1,0:T(8,128)(2,1)} %bitcast.19, f32[2560]{0:T(1024)} %refs_4_.1), custom_call_target="tpu_custom_call" | custom-call | flops 2621440 | bytes 2621440 | tf_op jit(solution)/shard_map/pallas_call | solution.py:107
  3.6 4.4 %all-to-all-start = ((bf16[4,2,5,2,64,128]{5,4,3,2,1,0:T(8,128)(2,1)}), bf16[4,2,5,2,64,128]{5,4,3,2,1,0:T(8,128)(2,1)S(1)}, u32[]{:S(2)}, u32[]{:S(2)}) async-start(bf16[4,2,5,2,64,128]{5,4,3,2,1,0:T(8,128)(2,1)} %shard_map.110), calls=%async_computation | async-start | bytes 2621440 | tf_op jit(solution)/shard_map/all_to_all | solution.py:461
  8.1 0.1 pad_dynamic-slice_fusion
  8.1 0.1 copy.12
  8.2 0.1 reshape.19
  8.3 0.6 pad_add_fusion.a
  9.0 3.0 %plan.1.refs_0_ = s32[64]{0:T(128)} custom-call(s32[145]{0:T(256)} %pad_add_fusion.a), custom_call_target="tpu_custom_call" | custom-call | flops 1000 | bytes 1000 | tf_op jit(solution)/shard_map/plan/pallas_call | solution.py:74
  12.0 13.9 %all-to-all-done.refs_1_ = bf16[4,2,5,2,64,128]{5,4,3,2,1,0:T(8,128)(2,1)S(1)} async-done(((bf16[4,2,5,2,64,128]{5,4,3,2,1,0:T(8,128)(2,1)}), bf16[4,2,5,2,64,128]{5,4,3,2,1,0:T(8,128)(2,1)S(1)}, u32[]{:S(2)}, u32[]{:S(2)}) %all-to-all-start) | async-done | bytes 1310752 | tf_op jit(solution)/shard_map/all_to_all | solution.py:461
  25.9 0.7 copy-done.5
  26.6 1.1 pack.1
  27.7 1.9 %collective-permute-start = (bf16[2,5,4,64,128]{4,3,2,1,0:T(8,128)(2,1)S(1)}, bf16[2,5,4,64,128]{4,3,2,1,0:T(8,128)(2,1)S(1)}, u32[]{:S(2)}, u32[]{:S(2)}) collective-permute-start(bf16[2,5,4,64,128]{4,3,2,1,0:T(8,128)(2,1)S(1)} %get-tuple-element.26), channel_id=1, source_target_pairs={{0,32},{32,64},{64,96},{96,128},{128,160},{160,192},{192,224},{224... | collective-permute-start | bytes 1966088 | tf_op jit(solution)/shard_map/ppermute | solution.py:467
  29.6 3.6 %collective-permute-start.1 = (bf16[2,5,4,64,128]{4,3,2,1,0:T(8,128)(2,1)S(1)}, bf16[2,5,4,64,128]{4,3,2,1,0:T(8,128)(2,1)S(1)}, u32[]{:S(2)}, u32[]{:S(2)}) collective-permute-start(bf16[2,5,4,64,128]{4,3,2,1,0:T(8,128)(2,1)S(1)} %get-tuple-element.27), channel_id=1, source_target_pairs={{32,0},{64,32},{96,64},{128,96},{160,128},{192,160},{224,192},{256... | collective-permute-start | bytes 1966088 | tf_op jit(solution)/shard_map/ppermute | solution.py:467
  33.3 1.8 %norm_query.1 = (bf16[2,5,2,64,128]{4,3,2,1,0:T(8,128)(2,1)S(1)}, bf16[2,5,2,64,128]{4,3,2,1,0:T(8,128)(2,1)S(1)}, bf16[2,5,2,64,128]{4,3,2,1,0:T(8,128)(2,1)S(1)}, bf16[2,5,2,64,128]{4,3,2,1,0:T(8,128)(2,1)S(1)}) custom-call(s32[64]{0:T(128)S(1)} %copy-done.5, bf16[128,2560]{1,0:T(8,128)(2,1)S(1)} %bitcast.15, bf16[128,2560]{1,0:T(8,128)(2,1)S(1)} %bitcast.17, ...), custom_call_target="tpu_custom_call" | custom-call | flops 2621440 | bytes 2621440 | tf_op jit(solution)/shard_map/norm_query/pallas_call | solution.py:150
  35.1 2.5 %collective-permute-start.2 = (bf16[2,5,2,64,128]{4,3,2,1,0:T(8,128)(2,1)S(1)}, bf16[2,5,2,64,128]{4,3,2,1,0:T(8,128)(2,1)S(1)}, u32[]{:S(2)}, u32[]{:S(2)}) collective-permute-start(bf16[2,5,2,64,128]{4,3,2,1,0:T(8,128)(2,1)S(1)} %get-tuple-element.29), channel_id=1, source_target_pairs={{0,8},{8,16},{16,24},{24,0},{1,9},{9,17},{17,25},{25,1},{2,10},{10... | collective-permute-start | bytes 983048 | tf_op jit(solution)/shard_map/ppermute | solution.py:472
  37.6 4.0 %collective-permute-start.3 = (bf16[2,5,2,64,128]{4,3,2,1,0:T(8,128)(2,1)S(1)}, bf16[2,5,2,64,128]{4,3,2,1,0:T(8,128)(2,1)S(1)}, u32[]{:S(2)}, u32[]{:S(2)}) collective-permute-start(bf16[2,5,2,64,128]{4,3,2,1,0:T(8,128)(2,1)S(1)} %get-tuple-element.30), channel_id=1, source_target_pairs={{0,16},{8,24},{16,0},{24,8},{1,17},{9,25},{17,1},{25,9},{2,18},{10... | collective-permute-start | bytes 983048 | tf_op jit(solution)/shard_map/ppermute | solution.py:472
  41.6 2.5 %collective-permute-start.4 = (bf16[2,5,2,64,128]{4,3,2,1,0:T(8,128)(2,1)S(1)}, bf16[2,5,2,64,128]{4,3,2,1,0:T(8,128)(2,1)S(1)}, u32[]{:S(2)}, u32[]{:S(2)}) collective-permute-start(bf16[2,5,2,64,128]{4,3,2,1,0:T(8,128)(2,1)S(1)} %get-tuple-element.31), channel_id=1, source_target_pairs={{0,24},{8,0},{16,8},{24,16},{1,25},{9,1},{17,9},{25,17},{2,26},{10... | collective-permute-start | bytes 983048 | tf_op jit(solution)/shard_map/ppermute | solution.py:472
  44.1 11.5 %collective-permute-done.2.refs_5_ = bf16[2,5,2,64,128]{4,3,2,1,0:T(8,128)(2,1)S(1)} collective-permute-done((bf16[2,5,2,64,128]{4,3,2,1,0:T(8,128)(2,1)S(1)}, bf16[2,5,2,64,128]{4,3,2,1,0:T(8,128)(2,1)S(1)}, u32[]{:S(2)}, u32[]{:S(2)}) %collective-permute-start.2) | collective-permute-done | bytes 327712 | tf_op jit(solution)/shard_map/ppermute | solution.py:472
  55.6 0.0 collective-permute-done.3.refs_6_
  55.6 2.9 %collective-permute-done.4.refs_7_ = bf16[2,5,2,64,128]{4,3,2,1,0:T(8,128)(2,1)S(1)} collective-permute-done((bf16[2,5,2,64,128]{4,3,2,1,0:T(8,128)(2,1)S(1)}, bf16[2,5,2,64,128]{4,3,2,1,0:T(8,128)(2,1)S(1)}, u32[]{:S(2)}, u32[]{:S(2)}) %collective-permute-start.4) | collective-permute-done | bytes 327712 | tf_op jit(solution)/shard_map/ppermute | solution.py:472
  58.5 0.0 copy-start.9
  58.6 0.8 copy-done.8
  59.4 0.2 copy-done.9
  59.6 12.2 %attend.1 = (bf16[4,5,2,64,128]{4,3,2,1,0:T(8,128)(2,1)S(1)}, bf16[4,2,5,2,64,128]{5,4,3,2,1,0:T(8,128)(2,1)}, bf16[2,5,4,64,128]{4,3,2,1,0:T(8,128)(2,1)S(1)}, ...) custom-call(s32[64]{0:T(128)S(1)} %copy-done.5, bf16[4,2,5,2,64,128]{5,4,3,2,1,0:T(8,128)(2,1)S(1)} %all-to-all-done.refs_1_, ...), custom_call_target="tpu_custom_call" | custom-call | flops 1509949440 | bytes 13107200 | tf_op jit(solution)/shard_map/attend/pallas_call | solution.py:429
  71.8 1.9 %collective-permute-start.5 = (bf16[2,5,4,64,128]{4,3,2,1,0:T(8,128)(2,1)S(1)}, bf16[2,5,4,64,128]{4,3,2,1,0:T(8,128)(2,1)S(1)}, u32[]{:S(2)}, u32[]{:S(2)}) collective-permute-start(bf16[2,5,4,64,128]{4,3,2,1,0:T(8,128)(2,1)S(1)} %get-tuple-element.34), channel_id=1, source_target_pairs={{32,0},{64,32},{96,64},{128,96},{160,128},{192,160},{224,192},{256... | collective-permute-start | bytes 1966088 | tf_op jit(solution)/shard_map/ppermute | solution.py:467
  73.7 2.4 %collective-permute-start.6 = (bf16[2,5,4,64,128]{4,3,2,1,0:T(8,128)(2,1)S(1)}, bf16[2,5,4,64,128]{4,3,2,1,0:T(8,128)(2,1)S(1)}, u32[]{:S(2)}, u32[]{:S(2)}) collective-permute-start(bf16[2,5,4,64,128]{4,3,2,1,0:T(8,128)(2,1)S(1)} %get-tuple-element.35), channel_id=1, source_target_pairs={{0,32},{32,64},{64,96},{96,128},{128,160},{160,192},{192,224},{224... | collective-permute-start | bytes 1966088 | tf_op jit(solution)/shard_map/ppermute | solution.py:467
  76.1 18.5 %all_to_all.15.refs_5_ = f32[8,16,128]{2,1,0:T(8,128)S(1)} all-to-all(f32[8,16,128]{2,1,0:T(8,128)S(1)} %get-tuple-element.36), channel_id=1, replica_groups=mesh['ctx'=16,'head'=4,'dp'=8] {'dp'}, dimensions={0} | all-to-all | bytes 131072 | tf_op jit(solution)/shard_map/all_to_all | solution.py:492
  94.6 0.0 collective-permute-done.5.refs_3_
  94.6 4.5 %merge.1 = (bf16[4,3,5,2,64,128]{5,4,3,2,1,0:T(8,128)(2,1)}, f32[16,128]{1,0:T(8,128)S(1)}) custom-call(s32[64]{0:T(128)S(1)} %copy-done.6, bf16[4,5,2,64,128]{4,3,2,1,0:T(8,128)(2,1)S(1)} %get-tuple-element.32.refs_1_, bf16[4,2,5,2,64,128]{5,4,3,2,1,0:T(8,128)(2,1)} %get-tuple-element.33.refs_2_, ...), custom_call_target="tpu_custom_call" | custom-call | flops 655360 | bytes 3932160 | tf_op jit(solution)/shard_map/merge/pallas_call | solution.py:299
  99.1 4.0 %all-to-all-start.2 = ((bf16[4,3,5,2,64,128]{5,4,3,2,1,0:T(8,128)(2,1)}), bf16[4,3,5,2,64,128]{5,4,3,2,1,0:T(8,128)(2,1)S(1)}, u32[]{:S(2)}, u32[]{:S(2)}) async-start(bf16[4,3,5,2,64,128]{5,4,3,2,1,0:T(8,128)(2,1)} %get-tuple-element.40), calls=%async_computation.2 | async-start | bytes 3932160 | tf_op jit(solution)/shard_map/all_to_all | solution.py:461
  103.1 15.7 %all-gather = f32[256,128]{1,0:T(8,128)S(1)} all-gather(f32[16,128]{1,0:T(8,128)S(1)} %get-tuple-element.41), channel_id=2, replica_groups=mesh['ctx'=16,'head'=4,'dp'=8] {'ctx'}, dimensions={0}, use_global_device_ids=true | all-gather | bytes 139264 | tf_op jit(solution)/shard_map/all_gather | solution.py:496
  118.8 15.6 %all-gather.1 = f32[64,128]{1,0:T(8,128)S(1)} all-gather(f32[16,128]{1,0:T(8,128)S(1)} %reduce_sum.9), channel_id=3, replica_groups=mesh['ctx'=16,'head'=4,'dp'=8] {'head'}, dimensions={0}, use_global_device_ids=true | all-gather | bytes 40960 | tf_op jit(solution)/shard_map/all_gather | solution.py:497
  134.4 2.7 %unnorm.1 = (bf16[128,2560]{1,0:T(8,128)(2,1)}, bf16[128,2560]{1,0:T(8,128)(2,1)}, bf16[128,2560]{1,0:T(8,128)(2,1)}, f32[2560]{0:T(1024)}, f32[2560]{0:T(1024)}) custom-call(bf16[128,2560]{1,0:T(8,128)(2,1)S(1)} %bitcast.16, bf16[128,2560]{1,0:T(8,128)(2,1)S(1)} %bitcast.14, bf16[4,3,5,2,64,128]{5,4,3,2,1,0:T(8,128)(2,1)S(1)} %all-to-all-done.2.refs_2_, ...), custom_call_target="tpu_custom_call" | custom-call | flops 7864320 | bytes 5242880 | tf_op jit(solution)/shard_map/unnorm/pallas_call | solution.py:223
  (23 shorter events, 0.1 us)
Async XLA Ops:
  3.6 4.4 %copy-start.7 = (s32[1,128,6]{1,0,2:T(1,128)S(1)}, s32[1,128,6]{1,0,2:T(1,128)}, u32[]{:S(2)}) copy-start(s32[1,128,6]{1,0,2:T(1,128)} %param.13) | copy-start | bytes 9220
  3.6 22.3 %all-to-all-start = ((bf16[4,2,5,2,64,128]{5,4,3,2,1,0:T(8,128)(2,1)}), bf16[4,2,5,2,64,128]{5,4,3,2,1,0:T(8,128)(2,1)S(1)}, u32[]{:S(2)}, u32[]{:S(2)}) async-start(bf16[4,2,5,2,64,128]{5,4,3,2,1,0:T(8,128)(2,1)} %shard_map.110), calls=%async_computation | async-start | bytes 2621440 | tf_op jit(solution)/shard_map/all_to_all | solution.py:461
  8.0 25.3 %copy-start.1 = (bf16[1,128,2560]{2,1,0:T(8,128)(2,1)S(1)}, bf16[1,128,2560]{2,1,0:T(8,128)(2,1)}, u32[]{:S(2)}) copy-start(bf16[1,128,2560]{2,1,0:T(8,128)(2,1)} %param.7) | copy-start | bytes 1966084
  8.0 25.3 %copy-start.2 = (bf16[1,128,2560]{2,1,0:T(8,128)(2,1)S(1)}, bf16[1,128,2560]{2,1,0:T(8,128)(2,1)}, u32[]{:S(2)}) copy-start(bf16[1,128,2560]{2,1,0:T(8,128)(2,1)} %param.10) | copy-start | bytes 1966084
  8.0 25.3 %copy-start.4 = (f32[2560]{0:T(1024)S(1)}, f32[2560]{0:T(1024)}, u32[]{:S(2)}) copy-start(f32[2560]{0:T(1024)} %refs_3_.3) | copy-start | bytes 30724
  25.9 0.7 copy-start.5
  27.7 30.8 %collective-permute-start = (bf16[2,5,4,64,128]{4,3,2,1,0:T(8,128)(2,1)S(1)}, bf16[2,5,4,64,128]{4,3,2,1,0:T(8,128)(2,1)S(1)}, u32[]{:S(2)}, u32[]{:S(2)}) collective-permute-start(bf16[2,5,4,64,128]{4,3,2,1,0:T(8,128)(2,1)S(1)} %get-tuple-element.26), channel_id=1, source_target_pairs={{0,32},{32,64},{64,96},{96,128},{128,160},{160,192},{192,224},{224... | collective-permute-start | bytes 1966088 | tf_op jit(solution)/shard_map/ppermute | solution.py:467
  29.6 28.9 %collective-permute-start.1 = (bf16[2,5,4,64,128]{4,3,2,1,0:T(8,128)(2,1)S(1)}, bf16[2,5,4,64,128]{4,3,2,1,0:T(8,128)(2,1)S(1)}, u32[]{:S(2)}, u32[]{:S(2)}) collective-permute-start(bf16[2,5,4,64,128]{4,3,2,1,0:T(8,128)(2,1)S(1)} %get-tuple-element.27), channel_id=1, source_target_pairs={{32,0},{64,32},{96,64},{128,96},{160,128},{192,160},{224,192},{256... | collective-permute-start | bytes 1966088 | tf_op jit(solution)/shard_map/ppermute | solution.py:467
  35.1 20.5 %collective-permute-start.2 = (bf16[2,5,2,64,128]{4,3,2,1,0:T(8,128)(2,1)S(1)}, bf16[2,5,2,64,128]{4,3,2,1,0:T(8,128)(2,1)S(1)}, u32[]{:S(2)}, u32[]{:S(2)}) collective-permute-start(bf16[2,5,2,64,128]{4,3,2,1,0:T(8,128)(2,1)S(1)} %get-tuple-element.29), channel_id=1, source_target_pairs={{0,8},{8,16},{16,24},{24,0},{1,9},{9,17},{17,25},{25,1},{2,10},{10... | collective-permute-start | bytes 983048 | tf_op jit(solution)/shard_map/ppermute | solution.py:472
  37.6 18.0 %collective-permute-start.3 = (bf16[2,5,2,64,128]{4,3,2,1,0:T(8,128)(2,1)S(1)}, bf16[2,5,2,64,128]{4,3,2,1,0:T(8,128)(2,1)S(1)}, u32[]{:S(2)}, u32[]{:S(2)}) collective-permute-start(bf16[2,5,2,64,128]{4,3,2,1,0:T(8,128)(2,1)S(1)} %get-tuple-element.30), channel_id=1, source_target_pairs={{0,16},{8,24},{16,0},{24,8},{1,17},{9,25},{17,1},{25,9},{2,18},{10... | collective-permute-start | bytes 983048 | tf_op jit(solution)/shard_map/ppermute | solution.py:472
  41.6 17.0 %collective-permute-start.4 = (bf16[2,5,2,64,128]{4,3,2,1,0:T(8,128)(2,1)S(1)}, bf16[2,5,2,64,128]{4,3,2,1,0:T(8,128)(2,1)S(1)}, u32[]{:S(2)}, u32[]{:S(2)}) collective-permute-start(bf16[2,5,2,64,128]{4,3,2,1,0:T(8,128)(2,1)S(1)} %get-tuple-element.31), channel_id=1, source_target_pairs={{0,24},{8,0},{16,8},{24,16},{1,25},{9,1},{17,9},{25,17},{2,26},{10... | collective-permute-start | bytes 983048 | tf_op jit(solution)/shard_map/ppermute | solution.py:472
  58.5 0.8 copy-start.8
  58.5 1.0 copy-start.9
  59.6 35.0 %copy-start.6 = (s32[64]{0:T(128)S(1)}, s32[64]{0:T(128)}, u32[]{:S(2)}) copy-start(s32[64]{0:T(128)} %plan.1.refs_0_) | copy-start | bytes 772
  71.8 22.8 %collective-permute-start.5 = (bf16[2,5,4,64,128]{4,3,2,1,0:T(8,128)(2,1)S(1)}, bf16[2,5,4,64,128]{4,3,2,1,0:T(8,128)(2,1)S(1)}, u32[]{:S(2)}, u32[]{:S(2)}) collective-permute-start(bf16[2,5,4,64,128]{4,3,2,1,0:T(8,128)(2,1)S(1)} %get-tuple-element.34), channel_id=1, source_target_pairs={{32,0},{64,32},{96,64},{128,96},{160,128},{192,160},{224,192},{256... | collective-permute-start | bytes 1966088 | tf_op jit(solution)/shard_map/ppermute | solution.py:467
  73.7 20.9 %collective-permute-start.6 = (bf16[2,5,4,64,128]{4,3,2,1,0:T(8,128)(2,1)S(1)}, bf16[2,5,4,64,128]{4,3,2,1,0:T(8,128)(2,1)S(1)}, u32[]{:S(2)}, u32[]{:S(2)}) collective-permute-start(bf16[2,5,4,64,128]{4,3,2,1,0:T(8,128)(2,1)S(1)} %get-tuple-element.35), channel_id=1, source_target_pairs={{0,32},{32,64},{64,96},{96,128},{128,160},{160,192},{192,224},{224... | collective-permute-start | bytes 1966088 | tf_op jit(solution)/shard_map/ppermute | solution.py:467
  99.1 35.3 %copy-start = (bf16[1,128,2560]{2,1,0:T(8,128)(2,1)S(1)}, bf16[1,128,2560]{2,1,0:T(8,128)(2,1)}, u32[]{:S(2)}) copy-start(bf16[1,128,2560]{2,1,0:T(8,128)(2,1)} %param.8) | copy-start | bytes 1966084
  99.1 35.3 %copy-start.3 = (f32[2560]{0:T(1024)S(1)}, f32[2560]{0:T(1024)}, u32[]{:S(2)}) copy-start(f32[2560]{0:T(1024)} %refs_4_.1) | copy-start | bytes 30724
  99.1 35.3 %all-to-all-start.2 = ((bf16[4,3,5,2,64,128]{5,4,3,2,1,0:T(8,128)(2,1)}), bf16[4,3,5,2,64,128]{5,4,3,2,1,0:T(8,128)(2,1)S(1)}, u32[]{:S(2)}, u32[]{:S(2)}) async-start(bf16[4,3,5,2,64,128]{5,4,3,2,1,0:T(8,128)(2,1)} %get-tuple-element.40), calls=%async_computation.2 | async-start | bytes 3932160 | tf_op jit(solution)/shard_map/all_to_all | solution.py:461
